TPU v7x, 128 devices: a whole 4x4x4 slice. The times are simulated.
128 devices in a mesh: cam: 4 (over y), tile: 32 (over z, x, core).
Axes of the slice: x: 4, y: 4, z: 4, core: 2. Of those that a mesh axis runs over, the one named last changes fastest.
Arguments:
- splat_params: float32 [59, 2097152], P(None, ('cam', 'tile'))
- first_moment: float32 [59, 2097152], P(None, ('cam', 'tile')), may hold values from -6 to 6
- second_moment: float32 [59, 2097152], P(None, ('cam', 'tile')), may hold values from 0.05 to 2
- camera_turn: float32 [4, 3], replicated, may hold values from -0.004 to 0.004
- camera_shift: float32 [4, 3], replicated, may hold values from -0.05 to 0.05
- fetch_table: int32 [128, 128, 128], P(('cam', 'tile')), may hold values from 0 to 16383, as said below
- tile_lists: int32 [4, 1024, 256], P('cam', 'tile'), may hold values from 0 to 16383, as said below
- tile_counts: int32 [4, 1024], P('cam', 'tile'), may hold values from 128 to 256, as said below
- tile_ids: int32 [4, 1024], P('cam', 'tile'), may hold values from 0 to 1023, as said below
- target_image: float32 [3, 4, 1024, 256], P(None, 'cam', 'tile'), may hold values from 0 to 1
Outputs:
- updated_params: float32 [59, 2097152], P(None, ('cam', 'tile'))
- updated_first: float32 [59, 2097152], P(None, ('cam', 'tile'))
- updated_second: float32 [59, 2097152], P(None, ('cam', 'tile'))
- rendered: float32 [3, 4, 1024, 256], P(None, 'cam', 'tile')
Inputs may be any that keep to these rules, and one draw needn't show every extreme that they name: `fetch_table`: for each source device, its entries over all rendering devices and slots name every one of its 16384 Gaussians exactly once. `tile_lists`: entries are slot numbers of the rendering device; no slot is named twice among all entries of the 32 tiles of one device. Live entries are in front-to-back order, and a Gaussian is named by at most one live entry of all lists. `tile_counts`: in every device one tile's list is full. `tile_ids`: for each camera, a permutation of its 1024 tile numbers.
All inputs are finite; a program needn't handle non-finite values.
Results may differ from a plain program's by a relative error of at most 0.0003.
Values sent between devices are 32-bit elements; how exact they have to be, the bound alone decides.
A program may use at most 192 MiB of HBM per device.

v0:
```python
import math

import jax
import jax.numpy as jnp
from jax import lax
from jax.sharding import PartitionSpec as P

TILE_PX = 16
GRID = 32


FOCAL = 512.0
CENTRE = 256.0
EYE_GAP = 20.0
DILATION = 0.3
SH_ZERO = 0.28209479177387814
SH_ONE = 0.4886025119029199
SH_TWO = (
    1.0925484305920792,
    -1.0925484305920792,
    0.31539156525252005,
    -1.0925484305920792,
    0.5462742152960396,
)
SH_THREE = (
    -0.5900435899266435,
    2.890611442640554,
    -0.4570457994644658,
    0.3731763325901154,
    -0.4570457994644658,
    1.445305721320277,
    -0.5900435899266435,
)
BETA_ONE = 0.9
BETA_TWO = 0.999
BIAS_ONE = 1.0 - math.exp(2000.0 * math.log(0.9))
BIAS_TWO = 1.0 - math.exp(2000.0 * math.log(0.999))
ADAM_EPS = 1e-08


def harmonics(dir_x, dir_y, dir_z):
    sq_x = dir_x * dir_x
    sq_y = dir_y * dir_y
    sq_z = dir_z * dir_z
    return [
        SH_ZERO * jnp.ones_like(dir_x),
        -SH_ONE * dir_y,
        SH_ONE * dir_z,
        -SH_ONE * dir_x,
        SH_TWO[0] * dir_x * dir_y,
        SH_TWO[1] * dir_y * dir_z,
        SH_TWO[2] * (2.0 * sq_z - sq_x - sq_y),
        SH_TWO[3] * dir_x * dir_z,
        SH_TWO[4] * (sq_x - sq_y),
        SH_THREE[0] * dir_y * (3.0 * sq_x - sq_y),
        SH_THREE[1] * dir_x * dir_y * dir_z,
        SH_THREE[2] * dir_y * (4.0 * sq_z - sq_x - sq_y),
        SH_THREE[3] * dir_z * (2.0 * sq_z - 3.0 * sq_x - 3.0 * sq_y),
        SH_THREE[4] * dir_x * (4.0 * sq_z - sq_x - sq_y),
        SH_THREE[5] * dir_z * (sq_x - sq_y),
        SH_THREE[6] * dir_x * (sq_x - 3.0 * sq_y),
    ]


def quat_matrix(quat_w, quat_x, quat_y, quat_z):
    return [
        [
            1.0 - 2.0 * (quat_y * quat_y + quat_z * quat_z),
            2.0 * (quat_x * quat_y - quat_w * quat_z),
            2.0 * (quat_x * quat_z + quat_w * quat_y),
        ],
        [
            2.0 * (quat_x * quat_y + quat_w * quat_z),
            1.0 - 2.0 * (quat_x * quat_x + quat_z * quat_z),
            2.0 * (quat_y * quat_z - quat_w * quat_x),
        ],
        [
            2.0 * (quat_x * quat_z - quat_w * quat_y),
            2.0 * (quat_y * quat_z + quat_w * quat_x),
            1.0 - 2.0 * (quat_x * quat_x + quat_y * quat_y),
        ],
    ]


def project(params, cam_quat, eye_pos):
    scales = [jnp.exp(params[3 + i]) for i in range(3)]
    norm_quat = jnp.sqrt(
        params[6] * params[6]
        + params[7] * params[7]
        + params[8] * params[8]
        + params[9] * params[9]
    )
    rotation = quat_matrix(
        params[6] / norm_quat, params[7] / norm_quat, params[8] / norm_quat, params[9] / norm_quat
    )
    camera = quat_matrix(cam_quat[0], cam_quat[1], cam_quat[2], cam_quat[3])
    relative = [params[i] - eye_pos[i] for i in range(3)]
    in_view = [
        camera[i][0] * relative[0] + camera[i][1] * relative[1] + camera[i][2] * relative[2]
        for i in range(3)
    ]
    inv_depth = 1.0 / in_view[2]
    screen_x = FOCAL * in_view[0] * inv_depth + CENTRE
    screen_y = FOCAL * in_view[1] * inv_depth + CENTRE
    axes_cam = [
        [
            (
                camera[i][0] * rotation[0][k]
                + camera[i][1] * rotation[1][k]
                + camera[i][2] * rotation[2][k]
            )
            * scales[k]
            for k in range(3)
        ]
        for i in range(3)
    ]
    slope_x = FOCAL * in_view[0] * inv_depth * inv_depth
    slope_y = FOCAL * in_view[1] * inv_depth * inv_depth
    row_x = [FOCAL * inv_depth * axes_cam[0][k] - slope_x * axes_cam[2][k] for k in range(3)]
    row_y = [FOCAL * inv_depth * axes_cam[1][k] - slope_y * axes_cam[2][k] for k in range(3)]
    cov_xx = row_x[0] * row_x[0] + row_x[1] * row_x[1] + row_x[2] * row_x[2] + DILATION
    cov_xy = row_x[0] * row_y[0] + row_x[1] * row_y[1] + row_x[2] * row_y[2]
    cov_yy = row_y[0] * row_y[0] + row_y[1] * row_y[1] + row_y[2] * row_y[2] + DILATION
    determinant = cov_xx * cov_yy - cov_xy * cov_xy
    distance = jnp.sqrt(
        relative[0] * relative[0] + relative[1] * relative[1] + relative[2] * relative[2]
    )
    basis = harmonics(relative[0] / distance, relative[1] / distance, relative[2] / distance)
    colours = []
    for channel in range(3):
        total = basis[0] * params[11 + channel]
        for k in range(1, 16):
            total = total + basis[k] * params[11 + 3 * k + channel]
        colours.append(jnp.maximum(total + 0.5, 0.0))
    opacity = jax.nn.sigmoid(params[10])
    return jnp.stack(
        [
            screen_x,
            screen_y,
            cov_yy / determinant,
            -cov_xy / determinant,
            cov_xx / determinant,
            colours[0],
            colours[1],
            colours[2],
            opacity,
        ]
    )


def camera_quats(camera_turn):
    norm_turn = jnp.sqrt(1.0 + jnp.sum(camera_turn * camera_turn, axis=1, keepdims=True))
    return jnp.concatenate([1.0 / norm_turn, camera_turn / norm_turn], axis=1)


def camera_eyes(camera_shift):
    survey = EYE_GAP * jnp.arange(camera_shift.shape[0]).astype(jnp.float32)
    return jnp.stack([survey + camera_shift[:, 0], camera_shift[:, 1], camera_shift[:, 2]], axis=1)


def pixel_centres(tile_numbers):
    pixel = jnp.arange(TILE_PX * TILE_PX)
    centre_x = (tile_numbers % GRID * TILE_PX)[:, None] + (pixel % TILE_PX)[None, :]
    centre_y = (tile_numbers // GRID * TILE_PX)[:, None] + (pixel // TILE_PX)[None, :]
    return (centre_x.astype(jnp.float32) + 0.5, centre_y.astype(jnp.float32) + 0.5)


def composite(records, counts, tile_numbers, prefix):
    centre_x, centre_y = pixel_centres(tile_numbers)
    offset_x = centre_x[:, :, None] - records[0][:, None, :]
    offset_y = centre_y[:, :, None] - records[1][:, None, :]
    exponent = (
        -0.5
        * (
            records[2][:, None, :] * offset_x * offset_x
            + records[4][:, None, :] * offset_y * offset_y
        )
        - records[3][:, None, :] * offset_x * offset_y
    )
    live = (jnp.arange(records.shape[2])[None, :] < counts[:, None]).astype(jnp.float32)
    alphas = records[8][:, None, :] * live[:, None, :] * jnp.exp(exponent)
    log_keep = jnp.log1p(-alphas)
    weights = jnp.exp(prefix(log_keep)) * alphas
    return jnp.einsum("bpk,cbk->cbp", weights, records[5:8], precision=lax.Precision.HIGHEST)


def adam(params, gradient, moment_one, moment_two):
    row_index = jnp.arange(params.shape[0])[:, None]
    step_sizes = jnp.where(
        row_index < 3,
        0.00016,
        jnp.where(
            row_index < 6,
            0.005,
            jnp.where(
                row_index < 10,
                0.001,
                jnp.where(row_index < 11, 0.025, jnp.where(row_index < 14, 0.0025, 0.000125)),
            ),
        ),
    )
    new_first = BETA_ONE * moment_one + (1.0 - BETA_ONE) * gradient
    new_second = BETA_TWO * moment_two + (1.0 - BETA_TWO) * gradient * gradient
    new_params = params - step_sizes * (new_first / BIAS_ONE) / (
        jnp.sqrt(new_second / BIAS_TWO) + ADAM_EPS
    )
    return (new_params, new_first, new_second)


def slot_tables(index, slots):
    inner = math.gcd(slots, 128)
    outer = slots // inner
    low_pick = (jnp.arange(inner, dtype=jnp.int32)[:, None] == (index % inner)[None, :]).astype(
        jnp.float32
    )
    high_pick = (jnp.arange(outer, dtype=jnp.int32)[:, None] == (index // inner)[None, :]).astype(
        jnp.float32
    )
    return (inner, outer, low_pick, high_pick)


def pick_slots(table, index):
    rows_here, slots = table.shape
    inner, outer, low_pick, high_pick = slot_tables(index, slots)
    partial_rows = jnp.einsum(
        "rab,be->rae",
        table.reshape(rows_here, outer, inner),
        low_pick,
        precision=lax.Precision.HIGHEST,
    )
    return jnp.sum(partial_rows * high_pick[None], axis=1)


def put_slots(values, index, slots):
    rows_here = values.shape[0]
    inner, outer, low_pick, high_pick = slot_tables(index, slots)
    spread = values[:, None, :] * high_pick[None]
    placed = jnp.einsum("rae,be->rab", spread, low_pick, precision=lax.Precision.HIGHEST)
    return placed.reshape(rows_here, slots)


def pick_columns(table, index):
    return jnp.transpose(jnp.take(jnp.transpose(table), index, axis=0))


def ask_sources(wanted):
    answer = lax.all_to_all(wanted, ("cam", "tile"), split_axis=0, concat_axis=0, tiled=True)
    return answer


def send_records(outgoing):
    answer = lax.all_to_all(outgoing, ("cam", "tile"), split_axis=1, concat_axis=1, tiled=True)
    return answer


def return_grads(incoming):
    answer = lax.all_to_all(incoming, ("cam", "tile"), split_axis=1, concat_axis=1, tiled=True)
    return answer


def render_tiles(records, lists_here, counts_here, ids_here, goal_here):
    tile_total, entries = lists_here.shape
    rows_rec, slots = records.shape
    per_step = 4
    groups = tile_total // per_step
    pixels = goal_here.shape[2]
    before_mask = (jnp.arange(entries)[:, None] < jnp.arange(entries)[None, :]).astype(jnp.float32)

    def prefix_sum(log_keep):
        return jnp.einsum("bpj,jk->bpk", log_keep, before_mask, precision=lax.Precision.HIGHEST)

    def tile_step(slot_total, block_in):
        block_lists, block_count, block_ids, block_goal = block_in
        flat_lists = block_lists.reshape(-1)
        gathered = pick_slots(records, flat_lists).reshape(rows_rec, per_step, entries)
        painted, pull_tiles = jax.vjp(
            lambda block_records: composite(block_records, block_count, block_ids, prefix_sum),
            gathered,
        )
        (rec_grad,) = pull_tiles(painted - block_goal)
        slot_total = slot_total + put_slots(rec_grad.reshape(rows_rec, -1), flat_lists, slots)
        return (slot_total, painted)

    blocks = (
        lists_here.reshape(groups, per_step, entries),
        counts_here.reshape(groups, per_step),
        ids_here.reshape(groups, per_step),
        jnp.moveaxis(goal_here.reshape(3, groups, per_step, pixels), 1, 0),
    )
    slot_grads, painted = lax.scan(tile_step, jnp.zeros((rows_rec, slots), jnp.float32), blocks)
    rendered = jnp.moveaxis(painted, 0, 1).reshape(3, tile_total, pixels)
    return (rendered, slot_grads)


def shards(
    splat_params,
    first_moment,
    second_moment,
    camera_turn,
    camera_shift,
    fetch_table,
    tile_lists,
    tile_counts,
    tile_ids,
    target_image,
):
    cam_count = lax.axis_size("cam")
    tile_count = lax.axis_size("tile")
    devices = cam_count * tile_count
    capacity = fetch_table.shape[2]
    own_count = splat_params.shape[1]
    rows_in = splat_params.shape[0]
    own_camera = lax.axis_index("cam")
    cam_quats = camera_quats(camera_turn)
    cam_eyes = camera_eyes(camera_shift)
    requested = ask_sources(fetch_table[0])
    flat_requested = requested.reshape(-1)
    order_count = flat_requested.shape[0]
    outgoing = pick_columns(splat_params, flat_requested).reshape(rows_in, devices, capacity)
    arrived = send_records(outgoing).reshape(rows_in, devices * capacity)
    records, pull_view = jax.vjp(
        lambda fetched: project(fetched, cam_quats[own_camera], cam_eyes[own_camera]), arrived
    )
    rendered, slot_grads = render_tiles(
        records, tile_lists[0], tile_counts[0], tile_ids[0], target_image[:, 0]
    )
    positions = jnp.arange(order_count, dtype=jnp.int32)
    (fetched_grads,) = pull_view(slot_grads)
    returned = return_grads(fetched_grads.reshape(rows_in, devices, capacity)).reshape(rows_in, -1)
    inverse = jnp.zeros((own_count,), jnp.int32).at[flat_requested].set(positions)
    gradient = pick_columns(returned, inverse)
    updated_params, updated_first, updated_second = adam(
        splat_params, gradient, first_moment, second_moment
    )
    return (updated_params, updated_first, updated_second, rendered[:, None])


def solution(mesh):
    return jax.shard_map(
        shards,
        mesh=mesh,
        in_specs=(
            P(None, ("cam", "tile")),
            P(None, ("cam", "tile")),
            P(None, ("cam", "tile")),
            P(),
            P(),
            P(("cam", "tile"), None, None),
            P("cam", "tile", None),
            P("cam", "tile"),
            P("cam", "tile"),
            P(None, "cam", "tile", None),
        ),
        out_specs=(
            P(None, ("cam", "tile")),
            P(None, ("cam", "tile")),
            P(None, ("cam", "tile")),
            P(None, "cam", "tile", None),
        ),
        check_vma=False,
    )
```

profile of v0, /device:TPU:1, one launch (start us, length us, event | category | flops | bytes accessed | tf_op | source)
XLA Modules:
  0.0 546.3 jit_solution(10344030429470943975)
XLA Ops:
  0.6 11.5 %all-to-all-start = ((s32[128,1,128]{2,1,0:T(1,128)}), s32[128,1,128]{2,1,0:T(1,128)S(1)}, u32[]{:S(2)}, u32[]{:S(2)}) async-start(s32[128,1,128]{2,1,0:T(1,128)} %bitcast.989), calls=%async_computation | async-start | bytes 131072 | tf_op jit(solution)/shard_map/all_to_all | solution.py:247
  12.1 7.0 %copy.113 = f32[59,16384]{0,1:T(8,128)} copy(f32[59,16384]{1,0:T(8,128)} %param.14) | data formatting | bytes 7733248 | tf_op args[0]
  21.6 58.2 %gather_fusion = f32[16384,59]{1,0:T(8,128)} fusion(f32[16384,59]{1,0:T(8,128)} %bitcast.926, s32[16384]{0:T(1024)S(1)} %fusion.88), kind=kCustom, calls=%fused_computation.clone | custom fusion | bytes 7798784 | tf_op jit(solution)/shard_map/jit(_take)/gather | solution.py:243
  79.9 13.1 %broadcast_select_fusion = f32[16384,59]{1,0:T(8,128)} fusion(f32[16384,59]{1,0:T(8,128)} %gather_fusion, pred[16384]{0:T(1024)(128)(4,1)S(1)} %compare_and_fusion.1), kind=kLoop, calls=%fused_computation.128 | loop fusion | flops 966656 | bytes 7749632 | tf_op jit(solution)/shard_map/jit(_take)/select_n | solution.py:243
  92.9 6.9 %copy.114 = f32[59,128,128]{2,0,1:T(8,128)} copy(f32[59,128,128]{0,2,1:T(8,128)} %bitcast.931) | data formatting | bytes 7733248 | tf_op jit(solution)/shard_map/reshape | solution.py:319
  99.8 8.5 %all-to-all-start.1 = ((f32[59,128,128]{2,0,1:T(8,128)}), f32[59,128,128]{2,0,1:T(8,128)}, u32[]{:S(2)}, u32[]{:S(2)}) async-start(f32[59,128,128]{2,0,1:T(8,128)} %copy.114), calls=%async_computation.1 | async-start | bytes 8388608 | tf_op jit(solution)/shard_map/all_to_all | solution.py:252
  125.2 35.6 %all-to-all-done.1 = f32[59,128,128]{2,0,1:T(8,128)} async-done(((f32[59,128,128]{2,0,1:T(8,128)}), f32[59,128,128]{2,0,1:T(8,128)}, u32[]{:S(2)}, u32[]{:S(2)}) %all-to-all-start.1) | async-done | bytes 3866656 | tf_op jit(solution)/shard_map/all_to_all | solution.py:252
  160.8 3.7 fusion.155
  169.7 4.5 fusion.150
  175.0 5.3 broadcast_maximum_fusion
  180.4 5.5 %broadcast_maximum_fusion.2 = (f32[1,16384]{1,0:T(1,128)S(1)}, f32[1,16384]{1,0:T(1,128)}) fusion(f32[1,16384]{1,0:T(1,128)S(1)} %get-tuple-element.318, f32[59,128,128]{2,0,1:T(8,128)} %all-to-all-done.1, f32[1,16384]{1,0:T(1,128)S(1)} %get-tuple-element.317, f32[1,16384]{1,0:T(1,128)S(1)} %get-tuple-element.313, f32[1,16384]{1,0:T(1,128)S(1)} %get-tuple-element.320, ...), kind=kLoop, calls=%fused_computation.335 | loop fusion | flops 884736 | bytes 1703936 | tf_op jit(solution)/shard_map/jvp()/max | solution.py:134
  185.8 5.3 broadcast_maximum_fusion.1
  192.2 145.3 %while.17 = (s32[]{:T(128)}, f32[9,16384]{1,0:T(8,128)S(1)}, f32[8,3,4,256]{3,1,2,0:T(4,128)}, s32[8,4,256]{2,1,0:T(4,128)}, f32[9,16384]{1,0:T(8,128)S(1)}, /*i...) while((s32[]{:T(128)}, f32[9,16384]{1,0:T(8,128)S(1)}, ...), condition=%wide.region_9.11_spmd.clone.clone, body=%wide.region_1.10_spmd.clone.clone.sunk | while | flops 5293194240 | bytes 17631056 | solution.py:290
  221.6 3.3 fusion.196
  344.6 3.4 sqrt_divide_fusion.6
  353.6 13.2 %multiply_add_fusion.12 = (f32[1,16384]{1,0:T(1,128)S(1)}, f32[1,16384]{1,0:T(1,128)S(1)}, f32[1,16384]{1,0:T(1,128)S(1)}, f32[1,16384]{1,0:T(1,128)S(1)}, f32[1...) fusion(f32[1,16384]{1,0:T(1,128)S(1)} %bitcast.969, f32[]{:T(128)} %bitcast.88, f32[]{:T(128)} %bitcast.87, ...), kind=kLoop, calls=%fused_computation.249 | loop fusion | flops 4096000 | bytes 5767180 | tf_op jit(solution)/shard_map/transpose(jvp())/add_any | solution.py:99
  376.8 12.1 %fusion.66 = f32[59,16384]{1,0:T(8,128)S(1)} fusion(f32[1,16384]{1,0:T(1,128)S(1)} %add_multiply_fusion.2, f32[1,16384]{1,0:T(1,128)S(1)} %get-tuple-element.427, f32[1,16384]{1,0:T(1,128)S(1)} %get-tuple-element.426, f32[1,16384]{1,0:T(1,128)S(1)} %get-tuple-element.377, f32[1,16384]{1,0:T(1,128)S(1)} %get-tuple-element.376, ...), kind=kLoop, calls=%fused_computation.124 | loop fusion | flops 63799296 | bytes 7995392 | tf_op jit(solution)/shard_map/transpose(jvp())/add_any | solution.py:86
  390.1 4.3 copy.175
  394.4 6.0 %all-to-all-start.2 = ((f32[59,128,128]{2,0,1:T(8,128)}), f32[59,128,128]{2,0,1:T(8,128)}, u32[]{:S(2)}, u32[]{:S(2)}) async-start(f32[59,128,128]{2,0,1:T(8,128)} %copy.175), calls=%async_computation.2 | async-start | bytes 8388608 | tf_op jit(solution)/shard_map/all_to_all | solution.py:257
  400.5 60.3 %scatter_custom_fusion = s32[16384]{0:T(1024)S(1)} fusion(s32[16384]{0:T(1024)S(1)} %bitcast.990, s32[16384]{0:T(1024)S(1)} %iota.78, s32[]{:T(128)} %constant.299.clone.1), kind=kCustom, calls=%fused_computation.328 | custom fusion | bytes 65540 | tf_op jit(solution)/shard_map/scatter | solution.py:330
  462.5 7.0 %copy.176 = f32[59,128,128]{0,2,1:T(8,128)} copy(f32[59,128,128]{2,0,1:T(8,128)} %all-to-all-done.2) | data formatting | bytes 7733248 | tf_op jit(solution)/shard_map/all_to_all | solution.py:257
  469.5 58.2 %gather_fusion.1 = f32[16384,59]{1,0:T(8,128)} fusion(f32[16384,59]{1,0:T(8,128)} %bitcast.927, s32[16384]{0:T(1024)S(1)} %fusion.89), kind=kCustom, calls=%fused_computation.1.clone | custom fusion | bytes 7798784 | tf_op jit(solution)/shard_map/jit(_take)/gather | solution.py:243
  527.8 6.8 %copy.177 = f32[16384,59]{0,1:T(8,128)} copy(f32[16384,59]{1,0:T(8,128)} %gather_fusion.1) | data formatting | bytes 7733248 | tf_op jit(solution)/shard_map/jit(_take)/gather | solution.py:243
  534.6 11.5 %divide_subtract_fusion = (f32[59,16384]{1,0:T(8,128)}, f32[59,16384]{1,0:T(8,128)}, f32[59,16384]{1,0:T(8,128)}) fusion(f32[59,16384]{1,0:T(8,128)} %param.14, f32[59]{0:T(128)S(1)} %compare_select_fusion.17, f32[16384,59]{0,1:T(8,128)} %copy.177, pred[16384]{0:T(1024)(128)(4,1)S(1)} %compare_and_fusion, f32[59,16384]{1,0:T(8,128)} %param.15, ...), kind=kLoop, calls=%fused_computation.129 | loop fusion | flops 12566528 | bytes 27082988 | tf_op jit(solution)/shard_map/sub | solution.py:204
  (510 shorter events, 179.3 us)
Async XLA Ops:
  0.6 20.9 %all-to-all-start = ((s32[128,1,128]{2,1,0:T(1,128)}), s32[128,1,128]{2,1,0:T(1,128)S(1)}, u32[]{:S(2)}, u32[]{:S(2)}) async-start(s32[128,1,128]{2,1,0:T(1,128)} %bitcast.989), calls=%async_computation | async-start | bytes 131072 | tf_op jit(solution)/shard_map/all_to_all | solution.py:247
  21.6 58.3 %copy-start.25 = (s32[128,1,128]{2,1,0:T(1,128)}, s32[128,1,128]{2,1,0:T(1,128)S(1)}, u32[]{:S(2)}) copy-start(s32[128,1,128]{2,1,0:T(1,128)S(1)} %all-to-all-done) | copy-start | bytes 196612
  99.8 21.2 %copy-start.54 = (f32[4,3]{1,0:T(4,128)S(1)}, f32[4,3]{1,0:T(4,128)}, u32[]{:S(2)}) copy-start(f32[4,3]{1,0:T(4,128)} %param.18) | copy-start | bytes 148
  99.8 21.8 %copy-start.55 = (s32[1,32]{1,0:T(1,128)S(1)}, s32[1,32]{1,0:T(1,128)}, u32[]{:S(2)}) copy-start(s32[1,32]{1,0:T(1,128)} %param.21) | copy-start | bytes 388
  99.8 22.6 %copy-start.56 = (s32[1,32]{1,0:T(1,128)S(1)}, s32[1,32]{1,0:T(1,128)}, u32[]{:S(2)}) copy-start(s32[1,32]{1,0:T(1,128)} %param.22) | copy-start | bytes 388
  99.8 23.3 %copy-start.51 = (f32[3,1,32,256]{3,2,1,0:T(8,128)S(1)}, f32[3,1,32,256]{3,2,1,0:T(8,128)}, u32[]{:S(2)}) copy-start(f32[3,1,32,256]{3,2,1,0:T(8,128)} %param.23) | copy-start | bytes 294916
  99.8 24.0 %copy-start.52 = (s32[1,32,256]{2,1,0:T(8,128)S(1)}, s32[1,32,256]{2,1,0:T(8,128)}, u32[]{:S(2)}) copy-start(s32[1,32,256]{2,1,0:T(8,128)} %param.20) | copy-start | bytes 98308
  99.8 61.0 %all-to-all-start.1 = ((f32[59,128,128]{2,0,1:T(8,128)}), f32[59,128,128]{2,0,1:T(8,128)}, u32[]{:S(2)}, u32[]{:S(2)}) async-start(f32[59,128,128]{2,0,1:T(8,128)} %copy.114), calls=%async_computation.1 | async-start | bytes 8388608 | tf_op jit(solution)/shard_map/all_to_all | solution.py:252
  166.0 14.3 %copy-start.2 = (f32[1,128,128]{2,1,0:T(8,128)}, f32[1,128,128]{2,1,0:T(8,128)S(1)}, u32[]{:S(2)}) copy-start(f32[1,128,128]{2,1,0:T(8,128)S(1)} %broadcast_subtract_fusion.1) | copy-start | bytes 196612
  166.6 13.7 %copy-start.13 = (f32[1,128,128]{2,1,0:T(8,128)}, f32[1,128,128]{2,1,0:T(8,128)S(1)}, u32[]{:S(2)}) copy-start(f32[1,128,128]{2,1,0:T(8,128)S(1)} %broadcast_subtract_fusion) | copy-start | bytes 196612
  174.4 17.8 %copy-start.32 = (f32[1,128,128]{2,1,0:T(8,128)}, f32[1,128,128]{2,1,0:T(8,128)S(1)}, u32[]{:S(2)}) copy-start(f32[1,128,128]{2,1,0:T(8,128)S(1)} %add_divide_fusion) | copy-start | bytes 196612
  180.3 10.9 %copy-start.5 = (f32[1,16384]{1,0:T(1,128)}, f32[1,16384]{1,0:T(1,128)S(1)}, u32[]{:S(2)}) copy-start(f32[1,16384]{1,0:T(1,128)S(1)} %get-tuple-element.313) | copy-start | bytes 196612
  180.3 10.9 %copy-start.7 = (f32[1,16384]{1,0:T(1,128)}, f32[1,16384]{1,0:T(1,128)S(1)}, u32[]{:S(2)}) copy-start(f32[1,16384]{1,0:T(1,128)S(1)} %get-tuple-element.317) | copy-start | bytes 196612
  337.5 11.9 %copy-start.48 = (f32[1,16384]{1,0:T(1,128)S(1)}, f32[1,16384]{1,0:T(1,128)}, u32[]{:S(2)}) copy-start(f32[1,16384]{1,0:T(1,128)} %get-tuple-element.360) | copy-start | bytes 196612
  337.5 11.9 %copy-start.49 = (f32[1,16384]{1,0:T(1,128)S(1)}, f32[1,16384]{1,0:T(1,128)}, u32[]{:S(2)}) copy-start(f32[1,16384]{1,0:T(1,128)} %get-tuple-element.361) | copy-start | bytes 196612
  337.5 11.9 %copy-start.50 = (f32[1,16384]{1,0:T(1,128)S(1)}, f32[1,16384]{1,0:T(1,128)}, u32[]{:S(2)}) copy-start(f32[1,16384]{1,0:T(1,128)} %get-tuple-element.362) | copy-start | bytes 196612
  337.5 12.2 %copy-start.6 = (f32[1,16384]{1,0:T(1,128)S(1)}, f32[1,16384]{1,0:T(1,128)}, u32[]{:S(2)}) copy-start(f32[1,16384]{1,0:T(1,128)} %copy-done.5) | copy-start | bytes 196612
  337.6 12.2 %copy-start.8 = (f32[1,16384]{1,0:T(1,128)S(1)}, f32[1,16384]{1,0:T(1,128)}, u32[]{:S(2)}) copy-start(f32[1,16384]{1,0:T(1,128)} %copy-done.7) | copy-start | bytes 196612
  337.6 12.2 %copy-start.10 = (f32[1,16384]{1,0:T(1,128)S(1)}, f32[1,16384]{1,0:T(1,128)}, u32[]{:S(2)}) copy-start(f32[1,16384]{1,0:T(1,128)} %copy-done.9) | copy-start | bytes 196612
  337.6 12.2 %copy-start.12 = (f32[1,16384]{1,0:T(1,128)S(1)}, f32[1,16384]{1,0:T(1,128)}, u32[]{:S(2)}) copy-start(f32[1,16384]{1,0:T(1,128)} %copy-done.11) | copy-start | bytes 196612
  337.6 12.2 %copy-start.17 = (f32[1,16384]{1,0:T(1,128)S(1)}, f32[1,16384]{1,0:T(1,128)}, u32[]{:S(2)}) copy-start(f32[1,16384]{1,0:T(1,128)} %copy-done.16) | copy-start | bytes 196612
  337.6 12.2 %copy-start.19 = (f32[1,16384]{1,0:T(1,128)S(1)}, f32[1,16384]{1,0:T(1,128)}, u32[]{:S(2)}) copy-start(f32[1,16384]{1,0:T(1,128)} %copy-done.18) | copy-start | bytes 196612
  337.6 12.2 %copy-start.21 = (f32[1,16384]{1,0:T(1,128)S(1)}, f32[1,16384]{1,0:T(1,128)}, u32[]{:S(2)}) copy-start(f32[1,16384]{1,0:T(1,128)} %copy-done.20) | copy-start | bytes 196612
  394.4 68.1 %all-to-all-start.2 = ((f32[59,128,128]{2,0,1:T(8,128)}), f32[59,128,128]{2,0,1:T(8,128)}, u32[]{:S(2)}, u32[]{:S(2)}) async-start(f32[59,128,128]{2,0,1:T(8,128)} %copy.175), calls=%async_computation.2 | async-start | bytes 8388608 | tf_op jit(solution)/shard_map/all_to_all | solution.py:257
  (36 other events, 296.6 us)
where the time goes:
time: 552 us; the launch traced here: 546 us
  local copies, waits for them, and re-layouts  235 us (43%)
  matrix products  123 us (22%)
  other arithmetic  109 us (20%)
  waiting for transfers between devices  38 us (7%)
  starting transfers between devices  26.1 us (5%)
  between operations  13.5 us (2%)
    gather x3, local copies, waits for them, and re-layouts, pick_columns(): return jnp.transpose(jnp.take(jnp.transpose(table), index, axis=0))  123 us
    scatter x1, local copies, waits for them, and re-layouts, shards(): jnp.zeros((own_count,), jnp.int32).at[flat_requested].set(positions)  60.3 us
    dot_general x24, matrix products, composite(): jnp.einsum('bpk,cbk->cbp', weights, records[5:8], precision=lax.Precision...  46.1 us
    dot_general x16, matrix products, prefix_sum(): jnp.einsum('bpj,jk->bpk', log_keep, before_mask, precision=lax.Precision....  40 us
    all_to_all x1, waiting for transfers between devices, send_records(): lax.all_to_all(outgoing, ('cam', 'tile'), split_axis=1, concat_axis=1, ti...  35.6 us
    dot_general x8, matrix products, put_slots(): jnp.einsum('rae,be->rab', spread, low_pick, precision=lax.Precision.HIGHEST)  19.6 us
    dot_general x8, matrix products, pick_slots(): jnp.einsum('rab,be->rae', table.reshape(rows_here, outer, inner), low_pic...  17.2 us
    max x3, other arithmetic, project(): colours.append(jnp.maximum(total + 0.5, 0.0))  16.1 us
  transfers between devices with their start and end apart: 3, of which 2 were waited for; matrix products, arithmetic and copies ran while one was open for 14% of the time, Pallas kernels for 0%

commit v1 on v0

v1 whole, which is shorter than its diff:
```python
import math

import jax
import jax.numpy as jnp
from jax import lax
from jax.experimental import pallas as pl
from jax.experimental.pallas import tpu as pltpu
from jax.sharding import PartitionSpec as P

TILE_PX = 16
GRID = 32


FOCAL = 512.0
CENTRE = 256.0
EYE_GAP = 20.0
DILATION = 0.3
SH_ZERO = 0.28209479177387814
SH_ONE = 0.4886025119029199
SH_TWO = (
    1.0925484305920792,
    -1.0925484305920792,
    0.31539156525252005,
    -1.0925484305920792,
    0.5462742152960396,
)
SH_THREE = (
    -0.5900435899266435,
    2.890611442640554,
    -0.4570457994644658,
    0.3731763325901154,
    -0.4570457994644658,
    1.445305721320277,
    -0.5900435899266435,
)
BETA_ONE = 0.9
BETA_TWO = 0.999
BIAS_ONE = 1.0 - math.exp(2000.0 * math.log(0.9))
BIAS_TWO = 1.0 - math.exp(2000.0 * math.log(0.999))
ADAM_EPS = 1e-08


def harmonics(dir_x, dir_y, dir_z):
    sq_x = dir_x * dir_x
    sq_y = dir_y * dir_y
    sq_z = dir_z * dir_z
    return [
        SH_ZERO * jnp.ones_like(dir_x),
        -SH_ONE * dir_y,
        SH_ONE * dir_z,
        -SH_ONE * dir_x,
        SH_TWO[0] * dir_x * dir_y,
        SH_TWO[1] * dir_y * dir_z,
        SH_TWO[2] * (2.0 * sq_z - sq_x - sq_y),
        SH_TWO[3] * dir_x * dir_z,
        SH_TWO[4] * (sq_x - sq_y),
        SH_THREE[0] * dir_y * (3.0 * sq_x - sq_y),
        SH_THREE[1] * dir_x * dir_y * dir_z,
        SH_THREE[2] * dir_y * (4.0 * sq_z - sq_x - sq_y),
        SH_THREE[3] * dir_z * (2.0 * sq_z - 3.0 * sq_x - 3.0 * sq_y),
        SH_THREE[4] * dir_x * (4.0 * sq_z - sq_x - sq_y),
        SH_THREE[5] * dir_z * (sq_x - sq_y),
        SH_THREE[6] * dir_x * (sq_x - 3.0 * sq_y),
    ]


def quat_matrix(quat_w, quat_x, quat_y, quat_z):
    return [
        [
            1.0 - 2.0 * (quat_y * quat_y + quat_z * quat_z),
            2.0 * (quat_x * quat_y - quat_w * quat_z),
            2.0 * (quat_x * quat_z + quat_w * quat_y),
        ],
        [
            2.0 * (quat_x * quat_y + quat_w * quat_z),
            1.0 - 2.0 * (quat_x * quat_x + quat_z * quat_z),
            2.0 * (quat_y * quat_z - quat_w * quat_x),
        ],
        [
            2.0 * (quat_x * quat_z - quat_w * quat_y),
            2.0 * (quat_y * quat_z + quat_w * quat_x),
            1.0 - 2.0 * (quat_x * quat_x + quat_y * quat_y),
        ],
    ]

LOG2E = math.log2(math.e)
HALF = 64
WIDE = 256
LANES = 128
BIG = 3e38
DEAD = -1e4
KEEP_MIN = 2.0**-24
BF = jnp.bfloat16
F32 = jnp.float32


def project(params, camera, eye_pos):
    scales = [jnp.exp(params[3 + i]) for i in range(3)]
    norm_quat = jnp.sqrt(
        params[6] * params[6]
        + params[7] * params[7]
        + params[8] * params[8]
        + params[9] * params[9]
    )
    rotation = quat_matrix(
        params[6] / norm_quat, params[7] / norm_quat, params[8] / norm_quat, params[9] / norm_quat
    )
    relative = [params[i] - eye_pos[i] for i in range(3)]
    in_view = [
        camera[i][0] * relative[0] + camera[i][1] * relative[1] + camera[i][2] * relative[2]
        for i in range(3)
    ]
    inv_depth = 1.0 / in_view[2]
    screen_x = FOCAL * in_view[0] * inv_depth + CENTRE
    screen_y = FOCAL * in_view[1] * inv_depth + CENTRE
    axes_cam = [
        [
            (
                camera[i][0] * rotation[0][k]
                + camera[i][1] * rotation[1][k]
                + camera[i][2] * rotation[2][k]
            )
            * scales[k]
            for k in range(3)
        ]
        for i in range(3)
    ]
    slope_x = FOCAL * in_view[0] * inv_depth * inv_depth
    slope_y = FOCAL * in_view[1] * inv_depth * inv_depth
    row_x = [FOCAL * inv_depth * axes_cam[0][k] - slope_x * axes_cam[2][k] for k in range(3)]
    row_y = [FOCAL * inv_depth * axes_cam[1][k] - slope_y * axes_cam[2][k] for k in range(3)]
    cov_xx = row_x[0] * row_x[0] + row_x[1] * row_x[1] + row_x[2] * row_x[2] + DILATION
    cov_xy = row_x[0] * row_y[0] + row_x[1] * row_y[1] + row_x[2] * row_y[2]
    cov_yy = row_y[0] * row_y[0] + row_y[1] * row_y[1] + row_y[2] * row_y[2] + DILATION
    inv_det = 1.0 / (cov_xx * cov_yy - cov_xy * cov_xy)
    inv_dist = 1.0 / jnp.sqrt(
        relative[0] * relative[0] + relative[1] * relative[1] + relative[2] * relative[2]
    )
    basis = harmonics(relative[0] * inv_dist, relative[1] * inv_dist, relative[2] * inv_dist)
    colours = []
    for channel in range(3):
        total = basis[0] * params[11 + channel]
        for k in range(1, 16):
            total = total + basis[k] * params[11 + 3 * k + channel]
        colours.append(jnp.maximum(total + 0.5, 0.0))
    return [
        screen_x,
        screen_y,
        cov_yy * inv_det,
        -cov_xy * inv_det,
        cov_xx * inv_det,
        colours[0],
        colours[1],
        colours[2],
    ]


def camera_of(turn_ref, shift_ref, cam, shape):
    turn = [jnp.full(shape, turn_ref[cam, i], F32) for i in range(3)]
    norm = jnp.sqrt(1.0 + (turn[0] * turn[0] + turn[1] * turn[1] + turn[2] * turn[2]))
    matrix = quat_matrix(1.0 / norm, turn[0] / norm, turn[1] / norm, turn[2] / norm)
    eye = [jnp.full(shape, shift_ref[cam, i], F32) for i in range(3)]
    eye[0] = EYE_GAP * cam + eye[0]
    return matrix, eye


def dense_rows(ref, columns):
    rows = []
    total = ref.shape[0]
    for start in range(0, total, 8):
        size = min(8, total - start)
        block = ref[start : start + size, :].reshape(size, columns // LANES, LANES)
        rows.extend(block[r] for r in range(size))
    return rows


def two_parts(value):
    high = value.astype(BF)
    return high, (value - high.astype(F32)).astype(BF)


def nt_dot(lhs, rhs):
    return lax.dot_general(lhs, rhs, (((1,), (1,)), ((), ())), preferred_element_type=F32)


def tn_dot(lhs, rhs):
    return lax.dot_general(lhs, rhs, (((0,), (0,)), ((), ())), preferred_element_type=F32)


def nn_dot(lhs, rhs):
    return lax.dot_general(lhs, rhs, (((1,), (0,)), ((), ())), preferred_element_type=F32)


def one_hots(index):
    count = index.shape[1]
    wide = (index >> 13) * LANES + (index & 127)
    narrow = (index >> 7) & 63
    pick = lax.broadcasted_iota(jnp.int32, (WIDE, count), 0) == wide
    mask = lax.broadcasted_iota(jnp.int32, (HALF, count), 0) == narrow
    return jnp.where(pick, 1.0, 0.0).astype(BF), jnp.where(mask, 1.0, 0.0)


def pick_from(table, low_table, index):
    pick, mask = one_hots(index)
    spread = nn_dot(table, jnp.concatenate([pick, pick], axis=0))
    extra = nn_dot(low_table, pick)
    picked = []
    for r in range(9):
        part = spread[r * HALF : (r + 1) * HALF]
        if r < 2:
            part = part + extra[r * HALF : (r + 1) * HALF]
        picked.append(jnp.sum(part * mask, axis=0, keepdims=True))
    return picked


def put_into(rows, index):
    pick, mask = one_hots(index)
    mask = mask.astype(BF)
    parts = [two_parts(row) for row in rows]
    high = jnp.concatenate([mask * part[0] for part in parts], axis=0)
    low = jnp.concatenate([mask * part[1] for part in parts], axis=0)
    return nt_dot(jnp.concatenate([high, low], axis=1), jnp.concatenate([pick, pick], axis=1))


def records_kernel(turn_ref, shift_ref, left_ref, right_ref, table_ref, low_ref):
    columns = left_ref.shape[1]
    rows = columns // LANES
    for half, ref in enumerate((left_ref, right_ref)):
        params = dense_rows(ref, columns)
        opacity = jax.nn.sigmoid(params[10])
        for cam in range(4):
            matrix, eye = camera_of(turn_ref, shift_ref, cam, (rows, LANES))
            record = project(params, matrix, eye) + [opacity]
            for r, value in enumerate(record):
                value = jnp.where(value == value, jnp.clip(value, -BIG, BIG), 0.0)
                high, mid = two_parts(value)
                at = half * LANES
                table_ref[cam, r, :, at : at + LANES] = high
                table_ref[cam, r, :, WIDE + at : WIDE + at + LANES] = mid
                if r < 2:
                    low = (value - high.astype(F32)) - mid.astype(F32)
                    low_ref[cam, r, :, at : at + LANES] = low.astype(BF)


def project_all(splat_params, camera_turn, camera_shift):
    rows_in, own_count = splat_params.shape
    columns = 2048
    steps = own_count // columns // 2
    rows = columns // LANES
    return pl.pallas_call(
        records_kernel,
        grid=(steps,),
        in_specs=[
            pl.BlockSpec(memory_space=pltpu.SMEM),
            pl.BlockSpec(memory_space=pltpu.SMEM),
            pl.BlockSpec((rows_in, columns), lambda i: (0, i)),
            pl.BlockSpec((rows_in, columns), lambda i: (0, i + steps)),
        ],
        out_specs=[
            pl.BlockSpec((4, 9, rows, 2 * WIDE), lambda i: (0, 0, i, 0)),
            pl.BlockSpec((4, 2, rows, WIDE), lambda i: (0, 0, i, 0)),
        ],
        out_shape=[
            jax.ShapeDtypeStruct((4, 9, HALF, 2 * WIDE), BF),
            jax.ShapeDtypeStruct((4, 2, HALF, WIDE), BF),
        ],
        compiler_params=pltpu.CompilerParams(vmem_limit_bytes=48 << 20),
        name="project_all",
    )(camera_turn, camera_shift, splat_params, splat_params)


def pair_of(ref, step):
    return jnp.concatenate([ref[pl.ds(2 * step, 1), :], ref[pl.ds(2 * step + 1, 1), :]], axis=1)


def answer_kernel(wanted_ref, table_ref, low_ref, out_ref):
    steps = wanted_ref.shape[0] // 2
    per_cam = steps // 4

    def body(step, carry):
        cam = step // per_cam
        picked = pick_from(
            table_ref[cam].reshape(9 * HALF, 2 * WIDE),
            low_ref[cam].reshape(2 * HALF, WIDE),
            pair_of(wanted_ref, step),
        )
        block = jnp.concatenate(picked, axis=0)
        out_ref[2 * step, 0:9, :] = block[:, :LANES]
        out_ref[2 * step + 1, 0:9, :] = block[:, LANES:]
        return carry

    lax.fori_loop(0, steps, body, 0, unroll=2)


def answer(wanted, table, low):
    devices, capacity = wanted.shape
    return pl.pallas_call(
        answer_kernel,
        in_specs=[pl.BlockSpec(memory_space=pltpu.VMEM)] * 3,
        out_specs=pl.BlockSpec(memory_space=pltpu.VMEM),
        out_shape=jax.ShapeDtypeStruct((devices, 16, capacity), F32),
        compiler_params=pltpu.CompilerParams(vmem_limit_bytes=48 << 20),
        name="answer",
    )(wanted, table, low)


def render_kernel(
    counts_ref, ids_ref, got_ref, lists_ref, goal_ref, image_ref, grads_ref,
    table_ref, low_ref, before_ref, after_ref, total_ref,
):
    tiles, entries = lists_ref.shape
    pixels = goal_ref.shape[2]

    for h in range(2):
        for r in range(9):
            value = jnp.concatenate(
                [got_ref[pl.ds((h * HALF + i) * 16 + r, 8, stride=16), :] for i in range(0, HALF, 8)], axis=0
            )
            high, mid = two_parts(value)
            table_ref[r * HALF : (r + 1) * HALF, h * LANES : (h + 1) * LANES] = high
            table_ref[r * HALF : (r + 1) * HALF, WIDE + h * LANES : WIDE + (h + 1) * LANES] = mid
            if r < 2:
                low = (value - high.astype(F32)) - mid.astype(F32)
                low_ref[r * HALF : (r + 1) * HALF, h * LANES : (h + 1) * LANES] = low.astype(BF)
    row = lax.broadcasted_iota(jnp.int32, (entries, entries), 0)
    col = lax.broadcasted_iota(jnp.int32, (entries, entries), 1)
    before_ref[...] = jnp.where(row < col, 1.0, 0.0).astype(BF)
    after_ref[...] = jnp.where(row > col, 1.0, 0.0).astype(BF)
    total_ref[...] = jnp.zeros_like(total_ref)

    def tile_step(tile):
        index = lists_ref[pl.ds(tile, 1), :]
        live = lax.broadcasted_iota(jnp.int32, (1, entries), 1) < counts_ref[0, tile]
        number = ids_ref[0, tile]
        origin_x = ((number & 31) * TILE_PX + TILE_PX // 2).astype(F32)
        origin_y = ((number >> 5) * TILE_PX + TILE_PX // 2).astype(F32)
        rec = pick_from(table_ref[...], low_ref[...], index)
        rec_u = jnp.where(live, rec[0] - origin_x, 0.0)
        rec_v = jnp.where(live, rec[1] - origin_y, 0.0)
        con_a = jnp.where(live, rec[2], 0.0)
        con_b = jnp.where(live, rec[3], 0.0)
        con_c = jnp.where(live, rec[4], 0.0)
        log_o = jnp.where(live, jnp.maximum(jnp.log(rec[8]) * LOG2E, DEAD), DEAD)
        colours = rec[5:8]

        spot = lax.broadcasted_iota(jnp.int32, (TILE_PX, entries), 0).astype(F32) - 7.5
        off_x = spot - rec_u
        off_y = spot - rec_v
        part_x = (-0.5 * LOG2E) * con_a * off_x * off_x + log_o
        cross = (-LOG2E) * con_b * off_x
        part_y = (-0.5 * LOG2E) * con_c * off_y * off_y
        power = jnp.concatenate(
            [part_x + (cross * off_y[y : y + 1] + part_y[y : y + 1]) for y in range(TILE_PX)], axis=0
        )
        alphas = jnp.exp2(power)
        log_keep = jnp.log(jnp.maximum(1.0 - alphas, KEEP_MIN))
        log_high, log_low = two_parts(log_keep)
        before = before_ref[...]
        after = after_ref[...]
        ahead = nn_dot(log_high, before) + nn_dot(log_low, before)
        weights = jnp.exp(ahead) * alphas
        w_high, w_low = two_parts(weights)

        col_parts = [two_parts(c) for c in colours]
        col_high = [p[0].astype(F32) for p in col_parts]
        col_low = [p[1].astype(F32) for p in col_parts]
        empty = [jnp.zeros((1, entries), F32)]
        col_stack = jnp.concatenate(col_high + col_low + empty * 10, axis=0).astype(BF)
        first = nt_dot(col_stack, w_high)
        second = nt_dot(col_stack, w_low)
        painted = [first[c : c + 1] + (first[3 + c : 4 + c] + second[c : c + 1]) for c in range(3)]
        residual = []
        for c in range(3):
            image_ref[c, pl.ds(tile, 1), :] = painted[c]
            residual.append(painted[c] - goal_ref[c, pl.ds(tile, 1), :])
        res_parts = [two_parts(c) for c in residual]
        res_high = [p[0].astype(F32) for p in res_parts]
        res_low = [p[1].astype(F32) for p in res_parts]
        blank = [jnp.zeros((1, pixels), F32)]
        res_left = jnp.concatenate(res_high + res_high + res_low + blank * 7, axis=0).astype(BF)
        col_right = jnp.concatenate(col_high + col_low + col_high + empty * 7, axis=0).astype(BF)
        weight_pull = tn_dot(res_left, col_right)
        res_stack = jnp.concatenate(res_high + res_low + blank * 10, axis=0).astype(BF)
        pull_one = nn_dot(res_stack, w_high)
        pull_two = nn_dot(res_stack, w_low)
        col_grads = [
            pull_one[c : c + 1] + (pull_one[3 + c : 4 + c] + pull_two[c : c + 1]) for c in range(3)
        ]
        share = weight_pull * weights
        s_high, s_low = two_parts(share)
        behind = nn_dot(s_high, after) + nn_dot(s_low, after)
        odds = jnp.exp2(power - log_keep * LOG2E)
        pull = share - odds * behind

        sum0 = jnp.zeros((TILE_PX, entries), F32)
        sum1 = sum0
        sum2 = sum0
        for y in range(TILE_PX - 1, -1, -1):
            sum0 = sum0 + pull[y * TILE_PX : (y + 1) * TILE_PX]
            sum1 = sum1 + sum0
            sum2 = sum2 + sum1
        first_y = sum1 - 8.5 * sum0
        second_y = 2.0 * sum2 - 18.0 * sum1 + 72.25 * sum0

        def over_x(value):
            return jnp.sum(value, axis=0, keepdims=True)

        m00 = over_x(sum0)
        m10 = over_x(spot * sum0)
        m20 = over_x(spot * spot * sum0)
        m01 = over_x(first_y)
        m11 = over_x(spot * first_y)
        m02 = over_x(second_y)
        by_x = m10 - rec_u * m00
        by_y = m01 - rec_v * m00
        by_xx = m20 - rec_u * (2.0 * m10 - rec_u * m00)
        by_xy = m11 - rec_u * m01 - rec_v * (m10 - rec_u * m00)
        by_yy = m02 - rec_v * (2.0 * m01 - rec_v * m00)
        grads = [
            con_a * by_x + con_b * by_y,
            con_c * by_y + con_b * by_x,
            -0.5 * by_xx,
            -by_xy,
            -0.5 * by_yy,
            col_grads[0],
            col_grads[1],
            col_grads[2],
            m00,
        ]
        total_ref[...] += put_into(grads, index)

    def body(step, carry):
        tile_step(step)
        return carry

    lax.fori_loop(0, tiles, body, 0)
    for h in range(2):
        for r in range(9):
            for i in range(0, HALF, 8):
                grads_ref[pl.ds((h * HALF + i) * 16 + r, 8, stride=16), :] = total_ref[
                    r * HALF + i : r * HALF + i + 8, h * LANES : (h + 1) * LANES
                ]


def render(counts, ids, got, lists, goal):
    tiles, entries = lists.shape
    vmem = pl.BlockSpec(memory_space=pltpu.VMEM)
    smem = pl.BlockSpec(memory_space=pltpu.SMEM)
    return pl.pallas_call(
        render_kernel,
        in_specs=[smem, smem, vmem, vmem, vmem],
        out_specs=[vmem, vmem],
        out_shape=[
            jax.ShapeDtypeStruct(goal.shape, F32),
            jax.ShapeDtypeStruct(got.shape, F32),
        ],
        scratch_shapes=[
            pltpu.VMEM((9 * HALF, 2 * WIDE), BF),
            pltpu.VMEM((2 * HALF, WIDE), BF),
            pltpu.VMEM((entries, entries), BF),
            pltpu.VMEM((entries, entries), BF),
            pltpu.VMEM((9 * HALF, WIDE), F32),
        ],
        compiler_params=pltpu.CompilerParams(vmem_limit_bytes=48 << 20),
        name="render",
    )(counts, ids, got, lists, goal)


def collect_kernel(wanted_ref, back_ref, out_ref, total_ref):
    steps = wanted_ref.shape[0] // 2
    per_cam = steps // 4
    total_ref[...] = jnp.zeros_like(total_ref)

    def body(step, carry):
        index = pair_of(wanted_ref, step)
        left = back_ref[2 * step, 0:9, :]
        right = back_ref[2 * step + 1, 0:9, :]
        block = jnp.concatenate([left, right], axis=1)
        viewer = jnp.full((1, WIDE), step // per_cam, jnp.int32).astype(F32)
        rows = [block[r : r + 1] for r in range(9)] + [viewer]
        total_ref[...] += put_into(rows, index)
        return carry

    lax.fori_loop(0, steps, body, 0, unroll=2)
    for r in range(10):
        for h in range(2):
            out_ref[r, h * HALF : (h + 1) * HALF, :] = total_ref[
                r * HALF : (r + 1) * HALF, h * LANES : (h + 1) * LANES
            ]


def collect(wanted, back):
    return pl.pallas_call(
        collect_kernel,
        in_specs=[pl.BlockSpec(memory_space=pltpu.VMEM)] * 2,
        out_specs=pl.BlockSpec(memory_space=pltpu.VMEM),
        out_shape=jax.ShapeDtypeStruct((10, 2 * HALF, LANES), F32),
        scratch_shapes=[pltpu.VMEM((10 * HALF, WIDE), F32)],
        compiler_params=pltpu.CompilerParams(vmem_limit_bytes=48 << 20),
        name="collect",
    )(wanted, back)


def step_size(row):
    if row < 3:
        return 0.00016
    if row < 6:
        return 0.005
    if row < 10:
        return 0.001
    if row < 11:
        return 0.025
    if row < 14:
        return 0.0025
    return 0.000125


def adam_kernel(turn_ref, shift_ref, pulls_ref, params_ref, one_ref, two_ref, new_ref, new_one_ref, new_two_ref):
    columns = params_ref.shape[1]
    total = params_ref.shape[0]
    rows = columns // LANES
    params = dense_rows(params_ref, columns)
    viewer = pulls_ref[9]
    matrix, eye = camera_of(turn_ref, shift_ref, 0, (rows, LANES))
    for cam in range(1, 4):
        here = viewer > cam - 0.5
        other, other_eye = camera_of(turn_ref, shift_ref, cam, (rows, LANES))
        matrix = [[jnp.where(here, other[i][j], matrix[i][j]) for j in range(3)] for i in range(3)]
        eye = [jnp.where(here, other_eye[i], eye[i]) for i in range(3)]
    _, pull_back = jax.vjp(lambda *values: project(values, matrix, eye), *params)
    grads = list(pull_back([pulls_ref[r] for r in range(8)]))
    grads[10] = pulls_ref[8] * jax.nn.sigmoid(-params[10])
    for start in range(0, total, 8):
        size = min(8, total - start)
        gradient = jnp.stack(grads[start : start + size], axis=0).reshape(size, columns)
        at = pl.ds(start, size)
        new_one = BETA_ONE * one_ref[at, :] + (1.0 - BETA_ONE) * gradient
        new_two = BETA_TWO * two_ref[at, :] + (1.0 - BETA_TWO) * gradient * gradient
        sizes = [step_size(row) / BIAS_ONE for row in range(start, start + size)]
        rate = jnp.full((size, 1), sizes[0], F32)
        which = lax.broadcasted_iota(jnp.int32, (size, 1), 0)
        for k in range(1, size):
            if sizes[k] != sizes[k - 1]:
                rate = jnp.where(which >= k, sizes[k], rate)
        new_one_ref[at, :] = new_one
        new_two_ref[at, :] = new_two
        new_ref[at, :] = params_ref[at, :] - rate * new_one / (
            jnp.sqrt(new_two * (1.0 / BIAS_TWO)) + ADAM_EPS
        )


def apply_adam(pulls, params, one, two, camera_turn, camera_shift):
    rows_in, own_count = params.shape
    columns = 1024
    block = pl.BlockSpec((rows_in, columns), lambda i: (0, i))
    return pl.pallas_call(
        adam_kernel,
        grid=(own_count // columns,),
        in_specs=[
            pl.BlockSpec(memory_space=pltpu.SMEM),
            pl.BlockSpec(memory_space=pltpu.SMEM),
            pl.BlockSpec((10, columns // LANES, LANES), lambda i: (0, i, 0)),
            block,
            block,
            block,
        ],
        out_specs=[block] * 3,
        out_shape=[jax.ShapeDtypeStruct(params.shape, F32)] * 3,
        compiler_params=pltpu.CompilerParams(vmem_limit_bytes=48 << 20),
        name="apply_adam",
    )(camera_turn, camera_shift, pulls, params, one, two)


def exchange(outgoing):
    return lax.all_to_all(outgoing, ("cam", "tile"), split_axis=0, concat_axis=0, tiled=True)


def shards(
    splat_params,
    first_moment,
    second_moment,
    camera_turn,
    camera_shift,
    fetch_table,
    tile_lists,
    tile_counts,
    tile_ids,
    target_image,
):
    devices, capacity = fetch_table.shape[1:]
    wanted = exchange(fetch_table[0])
    table, low = project_all(splat_params, camera_turn, camera_shift)
    arrived = exchange(answer(wanted, table, low))
    rendered, slot_grads = render(
        tile_counts, tile_ids, arrived.reshape(devices * 16, capacity), tile_lists[0], target_image[:, 0]
    )
    returned = exchange(slot_grads.reshape(devices, 16, capacity))
    pulls = collect(wanted, returned)
    updated_params, updated_first, updated_second = apply_adam(
        pulls, splat_params, first_moment, second_moment, camera_turn, camera_shift
    )
    return (updated_params, updated_first, updated_second, rendered[:, None])


def solution(mesh):
    return jax.shard_map(
        shards,
        mesh=mesh,
        in_specs=(
            P(None, ("cam", "tile")),
            P(None, ("cam", "tile")),
            P(None, ("cam", "tile")),
            P(),
            P(),
            P(("cam", "tile"), None, None),
            P("cam", "tile", None),
            P("cam", "tile"),
            P("cam", "tile"),
            P(None, "cam", "tile", None),
        ),
        out_specs=(
            P(None, ("cam", "tile")),
            P(None, ("cam", "tile")),
            P(None, ("cam", "tile")),
            P(None, "cam", "tile", None),
        ),
        check_vma=False,
    )
```

time: 552 us -> 183 us (0.33)
  local copies, waits for them, and re-layouts: 235 us -> 1.4 us
  matrix products: 123 us -> 0 us
  Pallas kernels: 0 us -> 116 us
  other arithmetic: 109 us -> 0 us
  blocking collectives: 0 us -> 50.2 us
  waiting for transfers between devices: 38 us -> 2.21 us
  starting transfers between devices: 26.1 us -> 11.5 us
  between operations: 13.5 us -> 0.77 us
    gather x3 -> x0, local copies, waits for them, and re-layouts: 123 us -> none  [pick_columns(): return jnp.transpose(jnp.take(jnp.transpose(table), index, axis=0))]
    dot_general x56 -> x0, matrix products: 123 us -> none  [the longest x24 46.1 us: composite(): jnp.einsum('bpk,cbk->cbp', weights, records[5:8], precision=lax.Precision...]
    pallas_call x0 -> x5, Pallas kernels: none -> 116 us  [the longest x1 60 us: render(): pl.pallas_call(render_kernel, in_specs=[smem, smem, vmem, vmem, vmem], ou...]
    scatter x1 -> x0, local copies, waits for them, and re-layouts: 60.3 us -> none  [shards(): jnp.zeros((own_count,), jnp.int32).at[flat_requested].set(positions)]
    all_to_all x0 -> x2, blocking collectives: none -> 50.2 us  [exchange(): lax.all_to_all(outgoing, ('cam', 'tile'), split_axis=0, concat_axis=0, ti...]
    all_to_all x3 -> x1, waiting for transfers between devices: 38 us -> 2.21 us  [exchange(): lax.all_to_all(outgoing, ('cam', 'tile'), split_axis=0, concat_axis=0, ti...]
    add_any x13 -> x0, other arithmetic: 29.6 us -> none  [the longest x1 13.2 us: project(): camera[i][2] * relative[2]]
    sub x5 -> x0, other arithmetic: 16.1 us -> none  [the longest x1 11.5 us: adam(): params - step_sizes * (new_first / BIAS_ONE) / (jnp.sqrt(new_second / BIA...]
  transfers between devices with their start and end apart: 3 -> 1, of which waited for: 2 -> 1; matrix products, arithmetic and copies ran while one was open for 14% -> 0% of each run, Pallas kernels for 0% -> 3%
where the time goes in v1:
time: 183 us; the launch traced here: 182 us
  Pallas kernels  116 us (63%)
  blocking collectives  50.2 us (27%)
  starting transfers between devices  11.5 us (6%)
  waiting for transfers between devices  2.21 us (1%)
    pallas_call x1, Pallas kernels, render(): pl.pallas_call(render_kernel, in_specs=[smem, smem, vmem, vmem, vmem], ou...  60 us
    all_to_all x2, blocking collectives, exchange(): lax.all_to_all(outgoing, ('cam', 'tile'), split_axis=0, concat_axis=0, ti...  50.2 us
    pallas_call x1, Pallas kernels, collect(): pl.pallas_call(collect_kernel, in_specs=[pl.BlockSpec(memory_space=pltpu....  18.7 us
    pallas_call x1, Pallas kernels, answer(): pl.pallas_call(answer_kernel, in_specs=[pl.BlockSpec(memory_space=pltpu.V...  17 us
    pallas_call x1, Pallas kernels, apply_adam(): pl.pallas_call(adam_kernel, grid=(own_count // columns,), in_specs=[pl.Bl...  14.7 us
    all_to_all x1, starting transfers between devices, exchange(): lax.all_to_all(outgoing, ('cam', 'tile'), split_axis=0, concat_axis=0, ti...  11.5 us
    pallas_call x1, Pallas kernels, project_all(): pl.pallas_call(records_kernel, grid=(steps,), in_specs=[pl.BlockSpec(memo...  5.79 us
  transfers between devices with their start and end apart: 1, of which 1 were waited for; matrix products, arithmetic and copies ran while one was open for 0% of the time, Pallas kernels for 3%

profile of v1, /device:TPU:1, one launch (start us, length us, event | category | flops | bytes accessed | tf_op | source)
XLA Modules:
  0.0 182.2 jit_solution(17951073274530321050)
XLA Ops:
  0.6 11.5 %all-to-all-start = ((s32[128,1,128]{2,1,0:T(1,128)}), s32[128,1,128]{2,1,0:T(1,128)S(1)}, u32[]{:S(2)}, u32[]{:S(2)}) async-start(s32[128,1,128]{2,1,0:T(1,128)} %bitcast.15), calls=%async_computation | async-start | bytes 131072 | tf_op jit(solution)/shard_map/all_to_all | solution.py:575
  12.1 0.0 copy-start.3
  12.2 0.7 copy-done.3
  12.8 0.7 copy-done.5
  13.5 5.8 %project_all.1 = (bf16[4,9,64,512]{3,2,1,0:T(8,128)(2,1)S(1)}, bf16[4,2,64,256]{3,2,1,0:T(8,128)(2,1)S(1)}) custom-call(f32[4,3]{1,0:T(4,128)S(1)} %copy-done.3, f32[4,3]{1,0:T(4,128)S(1)} %copy-done.5, f32[59,16384]{1,0:T(8,128)} %params_ref.1, f32[59,16384]{1,0:T(8,128)} %params_ref.1), custom_call_target="tpu_custom_call" | custom-call | tf_op jit(solution)/shard_map/project_all/pallas_call | solution.py:250
  19.3 0.0 copy-start.1
  19.3 0.0 copy-start.2
  19.3 0.0 copy-start.7
  19.3 0.0 copy-start.8
  19.3 2.2 %all-to-all-done = s32[128,1,128]{2,1,0:T(1,128)S(1)} async-done(((s32[128,1,128]{2,1,0:T(1,128)}), s32[128,1,128]{2,1,0:T(1,128)S(1)}, u32[]{:S(2)}, u32[]{:S(2)}) %all-to-all-start) | async-done | bytes 65568 | tf_op jit(solution)/shard_map/all_to_all | solution.py:575
  21.6 17.0 %answer.1 = f32[128,16,128]{2,1,0:T(8,128)S(1)} custom-call(s32[128,128]{1,0:T(8,128)S(1)} %bitcast.11, bf16[4,9,64,512]{3,2,1,0:T(8,128)(2,1)S(1)} %get-tuple-element.11.table_ref, bf16[4,2,64,256]{3,2,1,0:T(8,128)(2,1)S(1)} %get-tuple-element.12.low_ref), custom_call_target="tpu_custom_call" | custom-call | tf_op jit(solution)/shard_map/answer/pallas_call | solution.py:297
  38.5 0.0 copy-start
  38.5 0.0 copy-start.4
  38.6 0.0 copy-start.6
  38.6 26.7 %all_to_all.21 = f32[128,16,128]{2,1,0:T(8,128)S(1)} all-to-all(f32[128,16,128]{2,1,0:T(8,128)S(1)} %answer.1), channel_id=1, replica_groups=mesh['cam'=4,'tile'=32] {'cam','tile'}, dimensions={0} | all-to-all | bytes 2097152 | tf_op jit(solution)/shard_map/all_to_all | solution.py:575
  65.3 0.0 copy-done.1
  65.3 0.0 copy-done.2
  65.3 0.0 copy-done.7
  65.3 0.0 copy-done.8
  65.3 60.0 %render.1 = (f32[3,32,256]{2,1,0:T(8,128)}, f32[2048,128]{1,0:T(8,128)S(1)}) custom-call(s32[1,32]{1,0:T(1,128)S(1)} %copy-done.7, s32[1,32]{1,0:T(1,128)S(1)} %copy-done.8, f32[2048,128]{1,0:T(8,128)S(1)} %bitcast.9, s32[32,256]{1,0:T(8,128)S(1)} %bitcast.14, f32[3,32,256]{2,1,0:T(8,128)S(1)} %bitcast.13), custom_call_target="tpu_custom_call" | custom-call | tf_op jit(solution)/shard_map/render/pallas_call | solution.py:449
  125.3 23.5 %all_to_all.22.back_ref = f32[128,16,128]{2,1,0:T(8,128)S(1)} all-to-all(f32[128,16,128]{2,1,0:T(8,128)S(1)} %bitcast.10), channel_id=1, replica_groups=mesh['cam'=4,'tile'=32] {'cam','tile'}, dimensions={0} | all-to-all | bytes 2097152 | tf_op jit(solution)/shard_map/all_to_all | solution.py:575
  148.8 18.7 %collect.1.pulls_ref = f32[10,128,128]{2,1,0:T(8,128)S(1)} custom-call(s32[128,128]{1,0:T(8,128)S(1)} %bitcast.12, f32[128,16,128]{2,1,0:T(8,128)S(1)} %all_to_all.22.back_ref), custom_call_target="tpu_custom_call" | custom-call | tf_op jit(solution)/shard_map/collect/pallas_call | solution.py:493
  167.5 0.0 copy-done
  167.5 14.7 %apply_adam.1 = (f32[59,16384]{1,0:T(8,128)}, f32[59,16384]{1,0:T(8,128)}, f32[59,16384]{1,0:T(8,128)}) custom-call(f32[4,3]{1,0:T(4,128)S(1)} %copy-done.4, f32[4,3]{1,0:T(4,128)S(1)} %copy-done.6, f32[10,128,128]{2,1,0:T(8,128)S(1)} %collect.1.pulls_ref, f32[59,16384]{1,0:T(8,128)S(1)} %copy-done, f32[59,16384]{1,0:T(8,128)} %one_ref.1, f32[59,16384]{1,0:T(8,128)} %two_ref.1), custom_call_target="tpu_custom_call" | custom-call | tf_op jit(solution)/shard_map/apply_adam/pallas_call | solution.py:556
  (3 shorter events, 0.0 us)
Async XLA Ops:
  0.6 20.9 %all-to-all-start = ((s32[128,1,128]{2,1,0:T(1,128)}), s32[128,1,128]{2,1,0:T(1,128)S(1)}, u32[]{:S(2)}, u32[]{:S(2)}) async-start(s32[128,1,128]{2,1,0:T(1,128)} %bitcast.15), calls=%async_computation | async-start | bytes 131072 | tf_op jit(solution)/shard_map/all_to_all | solution.py:575
  12.1 0.7 copy-start.3
  12.8 0.7 copy-start.5
  19.3 46.0 %copy-start.1 = (f32[3,1,32,256]{3,2,1,0:T(8,128)S(1)}, f32[3,1,32,256]{3,2,1,0:T(8,128)}, u32[]{:S(2)}) copy-start(f32[3,1,32,256]{3,2,1,0:T(8,128)} %param.19) | copy-start | bytes 294916
  19.3 46.0 %copy-start.2 = (s32[1,32,256]{2,1,0:T(8,128)S(1)}, s32[1,32,256]{2,1,0:T(8,128)}, u32[]{:S(2)}) copy-start(s32[1,32,256]{2,1,0:T(8,128)} %param.16) | copy-start | bytes 98308
  19.3 46.0 %copy-start.7 = (s32[1,32]{1,0:T(1,128)S(1)}, s32[1,32]{1,0:T(1,128)}, u32[]{:S(2)}) copy-start(s32[1,32]{1,0:T(1,128)} %counts_ref.1) | copy-start | bytes 388
  19.3 46.0 %copy-start.8 = (s32[1,32]{1,0:T(1,128)S(1)}, s32[1,32]{1,0:T(1,128)}, u32[]{:S(2)}) copy-start(s32[1,32]{1,0:T(1,128)} %ids_ref.1) | copy-start | bytes 388
  38.5 129.0 %copy-start = (f32[59,16384]{1,0:T(8,128)S(1)}, f32[59,16384]{1,0:T(8,128)}, u32[]{:S(2)}) copy-start(f32[59,16384]{1,0:T(8,128)} %params_ref.1) | copy-start | bytes 11599876
  38.5 129.0 %copy-start.4 = (f32[4,3]{1,0:T(4,128)S(1)}, f32[4,3]{1,0:T(4,128)}, u32[]{:S(2)}) copy-start(f32[4,3]{1,0:T(4,128)} %turn_ref.3) | copy-start | bytes 148
  38.6 129.0 %copy-start.6 = (f32[4,3]{1,0:T(4,128)S(1)}, f32[4,3]{1,0:T(4,128)}, u32[]{:S(2)}) copy-start(f32[4,3]{1,0:T(4,128)} %shift_ref.3) | copy-start | bytes 148

commit v2 on v1

--- a/solution.py
+++ b/solution.py
@@ -1,3 +1,4 @@
+import functools
 import math
 
 import jax
@@ -193,11 +194,14 @@
 
 def one_hots(index):
     count = index.shape[1]
-    wide = (index >> 13) * LANES + (index & 127)
-    narrow = (index >> 7) & 63
-    pick = lax.broadcasted_iota(jnp.int32, (WIDE, count), 0) == wide
-    mask = lax.broadcasted_iota(jnp.int32, (HALF, count), 0) == narrow
-    return jnp.where(pick, 1.0, 0.0).astype(BF), jnp.where(mask, 1.0, 0.0)
+    wide = ((index >> 13) * LANES + (index & 127)).astype(F32).astype(BF)
+    narrow = ((index >> 7) & 63).astype(F32)
+    one = jnp.ones((), BF)
+    zero = jnp.zeros((), BF)
+    rows = lax.broadcasted_iota(jnp.int32, (WIDE, count), 0).astype(F32).astype(BF)
+    pick = jnp.where(rows == wide, one, zero)
+    few = lax.broadcasted_iota(jnp.int32, (HALF, count), 0).astype(F32)
+    return pick, jnp.where(few == narrow, 1.0, 0.0)
 
 
 def pick_from(table, low_table, index):
@@ -222,84 +226,194 @@
     return nt_dot(jnp.concatenate([high, low], axis=1), jnp.concatenate([pick, pick], axis=1))
 
 
-def records_kernel(turn_ref, shift_ref, left_ref, right_ref, table_ref, low_ref):
-    columns = left_ref.shape[1]
+MESH = pl.DeviceIdType.MESH
+
+
+def signal_all(barrier, cams, tiles):
+    own_cam = lax.axis_index("cam")
+    own_tile = lax.axis_index("tile")
+    for step in range(cams):
+        cam = lax.rem(own_cam + step, cams)
+
+        def tell(i, carry, cam=cam):
+            pl.semaphore_signal(
+                barrier, inc=1, device_id=(cam, lax.rem(own_tile + i, tiles)), device_id_type=MESH
+            )
+            return carry
+
+        lax.fori_loop(1 if step == 0 else 0, tiles, tell, 0, unroll=4)
+
+
+def project_block(turn_ref, shift_ref, params_ref, table_ref, low_ref, half, step, columns):
     rows = columns // LANES
-    for half, ref in enumerate((left_ref, right_ref)):
-        params = dense_rows(ref, columns)
-        opacity = jax.nn.sigmoid(params[10])
-        for cam in range(4):
-            matrix, eye = camera_of(turn_ref, shift_ref, cam, (rows, LANES))
-            record = project(params, matrix, eye) + [opacity]
-            for r, value in enumerate(record):
-                value = jnp.where(value == value, jnp.clip(value, -BIG, BIG), 0.0)
-                high, mid = two_parts(value)
-                at = half * LANES
-                table_ref[cam, r, :, at : at + LANES] = high
-                table_ref[cam, r, :, WIDE + at : WIDE + at + LANES] = mid
-                if r < 2:
-                    low = (value - high.astype(F32)) - mid.astype(F32)
-                    low_ref[cam, r, :, at : at + LANES] = low.astype(BF)
-
-
-def project_all(splat_params, camera_turn, camera_shift):
-    rows_in, own_count = splat_params.shape
+    start = pl.multiple_of(half * (HALF * LANES) + step * columns, columns)
+    params = []
+    total = params_ref.shape[0]
+    for first in range(0, total, 8):
+        size = min(8, total - first)
+        block = params_ref[first : first + size, pl.ds(start, columns)].reshape(size, rows, LANES)
+        params.extend(block[r] for r in range(size))
+    opacity = jax.nn.sigmoid(params[10])
+    at = half * LANES
+    place = pl.ds(pl.multiple_of(step * rows, rows), rows)
+    for cam in range(4):
+        matrix, eye = camera_of(turn_ref, shift_ref, cam, (rows, LANES))
+        record = project(params, matrix, eye) + [opacity]
+        for r, value in enumerate(record):
+            value = jnp.where(value == value, jnp.clip(value, -BIG, BIG), 0.0)
+            high, mid = two_parts(value)
+            table_ref[cam, r, place, at : at + LANES] = high
+            table_ref[cam, r, place, WIDE + at : WIDE + at + LANES] = mid
+            if r < 2:
+                low = (value - high.astype(F32)) - mid.astype(F32)
+                low_ref[cam, r, place, at : at + LANES] = low.astype(BF)
+
+
+def ask_kernel(
+    cams, tiles, turn_ref, shift_ref, fetch_ref, params_ref, wanted_ref, table_ref, low_ref,
+    held_ref, send_sem, recv_sem, own_sem, load_sem,
+):
     columns = 2048
-    steps = own_count // columns // 2
-    rows = columns // LANES
+    steps = HALF * LANES // columns
+    load = pltpu.make_async_copy(params_ref, held_ref, load_sem)
+    load.start()
+    barrier = pltpu.get_barrier_semaphore()
+    signal_all(barrier, cams, tiles)
+    own_cam = lax.axis_index("cam")
+    own_tile = lax.axis_index("tile")
+    me = own_cam * tiles + own_tile
+    others = cams * tiles - 1
+    own = pltpu.make_async_copy(fetch_ref.at[me], wanted_ref.at[me], own_sem)
+    own.start()
+    pl.semaphore_wait(barrier, others)
+    for hop in range(cams):
+        cam = lax.rem(own_cam + hop, cams)
+
+        def ask(i, carry, cam=cam):
+            tile = lax.rem(own_tile + i, tiles)
+            pltpu.make_async_remote_copy(
+                src_ref=fetch_ref.at[cam * tiles + tile],
+                dst_ref=wanted_ref.at[me],
+                send_sem=send_sem,
+                recv_sem=recv_sem,
+                device_id=(cam, tile),
+                device_id_type=MESH,
+            ).start()
+            return carry
+
+        lax.fori_loop(1 if hop == 0 else 0, tiles, ask, 0, unroll=4)
+    load.wait()
+
+    def body(step, carry):
+        for half in range(2):
+            project_block(turn_ref, shift_ref, held_ref, table_ref, low_ref, half, step, columns)
+        return carry
+
+    lax.fori_loop(0, steps, body, 0)
+    own.wait()
+    many = pl.ds(0, others)
+    pltpu.make_async_copy(fetch_ref.at[many], wanted_ref.at[many], send_sem).wait()
+    pltpu.make_async_copy(fetch_ref.at[many], wanted_ref.at[many], recv_sem).wait()
+
+
+def ask_and_project(mesh_shape, fetch, splat_params, camera_turn, camera_shift):
+    vmem = pl.BlockSpec(memory_space=pltpu.VMEM)
+    smem = pl.BlockSpec(memory_space=pltpu.SMEM)
     return pl.pallas_call(
-        records_kernel,
-        grid=(steps,),
-        in_specs=[
-            pl.BlockSpec(memory_space=pltpu.SMEM),
-            pl.BlockSpec(memory_space=pltpu.SMEM),
-            pl.BlockSpec((rows_in, columns), lambda i: (0, i)),
-            pl.BlockSpec((rows_in, columns), lambda i: (0, i + steps)),
-        ],
-        out_specs=[
-            pl.BlockSpec((4, 9, rows, 2 * WIDE), lambda i: (0, 0, i, 0)),
-            pl.BlockSpec((4, 2, rows, WIDE), lambda i: (0, 0, i, 0)),
-        ],
+        functools.partial(ask_kernel, *mesh_shape),
+        in_specs=[smem, smem, vmem, pl.BlockSpec(memory_space=pl.ANY)],
+        out_specs=[vmem] * 3,
         out_shape=[
+            jax.ShapeDtypeStruct(fetch.shape, jnp.int32),
             jax.ShapeDtypeStruct((4, 9, HALF, 2 * WIDE), BF),
             jax.ShapeDtypeStruct((4, 2, HALF, WIDE), BF),
         ],
-        compiler_params=pltpu.CompilerParams(vmem_limit_bytes=48 << 20),
-        name="project_all",
-    )(camera_turn, camera_shift, splat_params, splat_params)
-
-
-def pair_of(ref, step):
-    return jnp.concatenate([ref[pl.ds(2 * step, 1), :], ref[pl.ds(2 * step + 1, 1), :]], axis=1)
-
-
-def answer_kernel(wanted_ref, table_ref, low_ref, out_ref):
-    steps = wanted_ref.shape[0] // 2
-    per_cam = steps // 4
-
-    def body(step, carry):
-        cam = step // per_cam
+        scratch_shapes=[pltpu.VMEM(splat_params.shape, F32)] + [pltpu.SemaphoreType.DMA(())] * 4,
+        compiler_params=pltpu.CompilerParams(
+            vmem_limit_bytes=48 << 20, collective_id=0, has_side_effects=True
+        ),
+        name="ask_and_project",
+    )(camera_turn, camera_shift, fetch, splat_params)
+
+
+def pair_of(ref, chip):
+    return jnp.concatenate([ref[2 * chip], ref[2 * chip + 1]], axis=1)
+
+
+def answer_kernel(cams, tiles, wanted_ref, table_ref, low_ref, got_ref, held_ref, send_sem, recv_sem, own_sem):
+    chips = cams * tiles // 2
+    per_cam = chips // cams
+    others = 2 * chips - 1
+    me = lax.axis_index("cam") * tiles + lax.axis_index("tile")
+    own_chip = me // 2
+    twin = 2 * own_chip + (1 - lax.rem(me, 2))
+    barrier = pltpu.get_barrier_semaphore()
+    signal_all(barrier, cams, tiles)
+
+    def fill(chip):
         picked = pick_from(
-            table_ref[cam].reshape(9 * HALF, 2 * WIDE),
-            low_ref[cam].reshape(2 * HALF, WIDE),
-            pair_of(wanted_ref, step),
+            table_ref[chip // per_cam].reshape(9 * HALF, 2 * WIDE),
+            low_ref[chip // per_cam].reshape(2 * HALF, WIDE),
+            pair_of(wanted_ref, chip),
         )
         block = jnp.concatenate(picked, axis=0)
-        out_ref[2 * step, 0:9, :] = block[:, :LANES]
-        out_ref[2 * step + 1, 0:9, :] = block[:, LANES:]
+        held_ref[2 * chip, 0:9, :] = block[:, :LANES]
+        held_ref[2 * chip + 1, 0:9, :] = block[:, LANES:]
+
+    def send(other):
+        pltpu.make_async_remote_copy(
+            src_ref=held_ref.at[other, 0:9],
+            dst_ref=got_ref.at[me, 0:9],
+            send_sem=send_sem,
+            recv_sem=recv_sem,
+            device_id=(other // tiles, lax.rem(other, tiles)),
+            device_id_type=MESH,
+        ).start()
+
+    per_batch = 4
+
+    def fill_batch(batch):
+        for k in range(per_batch):
+            fill(lax.rem(own_chip + batch * per_batch + k, chips))
+
+    def send_chip(step):
+        chip = lax.rem(own_chip + step, chips)
+        send(2 * chip)
+        send(2 * chip + 1)
+
+    fill_batch(0)
+    own = pltpu.make_async_copy(held_ref.at[me, 0:9], got_ref.at[me, 0:9], own_sem)
+    own.start()
+    pl.semaphore_wait(barrier, others)
+    send(twin)
+    for k in range(1, per_batch):
+        send_chip(k)
+
+    def body(batch, carry):
+        fill_batch(batch)
+        for k in range(per_batch):
+            send_chip(batch * per_batch + k)
         return carry
 
-    lax.fori_loop(0, steps, body, 0, unroll=2)
-
-
-def answer(wanted, table, low):
-    devices, capacity = wanted.shape
+    lax.fori_loop(1, chips // per_batch, body, 0)
+    own.wait()
+    many = pl.ds(0, others)
+    pltpu.make_async_copy(held_ref.at[many, 0:9], got_ref.at[many, 0:9], send_sem).wait()
+    pltpu.make_async_copy(held_ref.at[many, 0:9], got_ref.at[many, 0:9], recv_sem).wait()
+
+
+def answer(mesh_shape, wanted, table, low):
+    devices, _, capacity = wanted.shape
+    shape = (devices, 16, capacity)
     return pl.pallas_call(
-        answer_kernel,
+        functools.partial(answer_kernel, *mesh_shape),
         in_specs=[pl.BlockSpec(memory_space=pltpu.VMEM)] * 3,
         out_specs=pl.BlockSpec(memory_space=pltpu.VMEM),
-        out_shape=jax.ShapeDtypeStruct((devices, 16, capacity), F32),
-        compiler_params=pltpu.CompilerParams(vmem_limit_bytes=48 << 20),
+        out_shape=jax.ShapeDtypeStruct(shape, F32),
+        scratch_shapes=[pltpu.VMEM(shape, F32)] + [pltpu.SemaphoreType.DMA(())] * 3,
+        compiler_params=pltpu.CompilerParams(
+            vmem_limit_bytes=48 << 20, collective_id=1, has_side_effects=True
+        ),
         name="answer",
     )(wanted, table, low)
 
@@ -433,7 +547,7 @@
         tile_step(step)
         return carry
 
-    lax.fori_loop(0, tiles, body, 0)
+    lax.fori_loop(0, tiles, body, 0, unroll=2)
     for h in range(2):
         for r in range(9):
             for i in range(0, HALF, 8):
@@ -466,39 +580,83 @@
     )(counts, ids, got, lists, goal)
 
 
-def collect_kernel(wanted_ref, back_ref, out_ref, total_ref):
-    steps = wanted_ref.shape[0] // 2
-    per_cam = steps // 4
+def collect_kernel(
+    cams, tiles, wanted_ref, away_ref, out_ref, back_ref, total_ref, send_sem, recv_sem
+):
+    chips = cams * tiles // 2
+    per_cam = chips // cams
+    per_group = 4
+    groups = chips // per_group
+    others = 2 * chips - 1
+    me = lax.axis_index("cam") * tiles + lax.axis_index("tile")
+    own_chip = me // 2
+    twin = 2 * own_chip + (1 - lax.rem(me, 2))
+    barrier = pltpu.get_barrier_semaphore()
+    signal_all(barrier, cams, tiles)
+    own = pltpu.make_async_copy(away_ref.at[me, 0:9], back_ref.at[me, 0:9], recv_sem.at[0])
+    own.start()
     total_ref[...] = jnp.zeros_like(total_ref)
-
-    def body(step, carry):
-        index = pair_of(wanted_ref, step)
-        left = back_ref[2 * step, 0:9, :]
-        right = back_ref[2 * step + 1, 0:9, :]
-        block = jnp.concatenate([left, right], axis=1)
-        viewer = jnp.full((1, WIDE), step // per_cam, jnp.int32).astype(F32)
-        rows = [block[r : r + 1] for r in range(9)] + [viewer]
-        total_ref[...] += put_into(rows, index)
+    pl.semaphore_wait(barrier, others)
+
+    def send(other, group):
+        pltpu.make_async_remote_copy(
+            src_ref=away_ref.at[other, 0:9],
+            dst_ref=back_ref.at[me, 0:9],
+            send_sem=send_sem,
+            recv_sem=recv_sem.at[group],
+            device_id=(other // tiles, lax.rem(other, tiles)),
+            device_id_type=MESH,
+        ).start()
+
+    send(twin, 0)
+
+    def give(step, carry):
+        chip = lax.rem(own_chip + step, chips)
+        send(2 * chip, step // per_group)
+        send(2 * chip + 1, step // per_group)
         return carry
 
-    lax.fori_loop(0, steps, body, 0, unroll=2)
+    lax.fori_loop(1, chips, give, 0, unroll=3)
+
+    def take(group, carry):
+        block = pl.ds(0, 2 * per_group)
+        pltpu.make_async_copy(away_ref.at[block, 0:9], back_ref.at[block, 0:9], recv_sem.at[group]).wait()
+        for k in range(per_group):
+            chip = lax.rem(own_chip + chips - (group * per_group + k), chips)
+            both = jnp.concatenate([back_ref[2 * chip, 0:9, :], back_ref[2 * chip + 1, 0:9, :]], axis=1)
+            viewer = jnp.full((1, WIDE), chip // per_cam, jnp.int32).astype(F32)
+            rows = [both[r : r + 1] for r in range(9)] + [viewer]
+            total_ref[...] += put_into(rows, pair_of(wanted_ref, chip))
+        return carry
+
+    lax.fori_loop(0, groups, take, 0)
     for r in range(10):
         for h in range(2):
             out_ref[r, h * HALF : (h + 1) * HALF, :] = total_ref[
                 r * HALF : (r + 1) * HALF, h * LANES : (h + 1) * LANES
             ]
-
-
-def collect(wanted, back):
+    many = pl.ds(0, others)
+    pltpu.make_async_copy(away_ref.at[many, 0:9], back_ref.at[many, 0:9], send_sem).wait()
+
+
+def collect(mesh_shape, wanted, away):
+    chips = mesh_shape[0] * mesh_shape[1] // 2
     return pl.pallas_call(
-        collect_kernel,
+        functools.partial(collect_kernel, *mesh_shape),
         in_specs=[pl.BlockSpec(memory_space=pltpu.VMEM)] * 2,
         out_specs=pl.BlockSpec(memory_space=pltpu.VMEM),
         out_shape=jax.ShapeDtypeStruct((10, 2 * HALF, LANES), F32),
-        scratch_shapes=[pltpu.VMEM((10 * HALF, WIDE), F32)],
-        compiler_params=pltpu.CompilerParams(vmem_limit_bytes=48 << 20),
+        scratch_shapes=[
+            pltpu.VMEM(away.shape, F32),
+            pltpu.VMEM((10 * HALF, WIDE), F32),
+            pltpu.SemaphoreType.DMA(()),
+            pltpu.SemaphoreType.DMA((chips // 4,)),
+        ],
+        compiler_params=pltpu.CompilerParams(
+            vmem_limit_bytes=48 << 20, collective_id=2, has_side_effects=True
+        ),
         name="collect",
-    )(wanted, back)
+    )(wanted, away)
 
 
 def step_size(row):
@@ -571,10 +729,6 @@
     )(camera_turn, camera_shift, pulls, params, one, two)
 
 
-def exchange(outgoing):
-    return lax.all_to_all(outgoing, ("cam", "tile"), split_axis=0, concat_axis=0, tiled=True)
-
-
 def shards(
     splat_params,
     first_moment,
@@ -588,14 +742,15 @@
     target_image,
 ):
     devices, capacity = fetch_table.shape[1:]
-    wanted = exchange(fetch_table[0])
-    table, low = project_all(splat_params, camera_turn, camera_shift)
-    arrived = exchange(answer(wanted, table, low))
+    mesh_shape = (lax.axis_size("cam"), lax.axis_size("tile"))
+    wanted, table, low = ask_and_project(
+        mesh_shape, fetch_table.reshape(devices, 1, capacity), splat_params, camera_turn, camera_shift
+    )
+    arrived = answer(mesh_shape, wanted, table, low)
     rendered, slot_grads = render(
         tile_counts, tile_ids, arrived.reshape(devices * 16, capacity), tile_lists[0], target_image[:, 0]
     )
-    returned = exchange(slot_grads.reshape(devices, 16, capacity))
-    pulls = collect(wanted, returned)
+    pulls = collect(mesh_shape, wanted, slot_grads.reshape(devices, 16, capacity))
     updated_params, updated_first, updated_second = apply_adam(
         pulls, splat_params, first_moment, second_moment, camera_turn, camera_shift
     )

time: 183 us -> 142 us (0.78)
  blocking collectives: 50.2 us -> 0 us
  Pallas kernels: 116 us -> 138 us
  starting transfers between devices: 11.5 us -> 0 us
  waiting for transfers between devices: 2.21 us -> 0 us
    all_to_all x2 -> x0, blocking collectives: 50.2 us -> none  [exchange(): lax.all_to_all(outgoing, ('cam', 'tile'), split_axis=0, concat_axis=0, ti...]
    pallas_call x3, Pallas kernels: 41.5 us -> 67.1 us  [the longest x1 27.1 us: collect(): pl.pallas_call(functools.partial(collect_kernel, *mesh_shape), in_specs=[...]
    all_to_all x1 -> x0, starting transfers between devices: 11.5 us -> none  [exchange(): lax.all_to_all(outgoing, ('cam', 'tile'), split_axis=0, concat_axis=0, ti...]
    pallas_call x1, Pallas kernels: 60 us -> 56.4 us  [render(): pl.pallas_call(render_kernel, in_specs=[smem, smem, vmem, vmem, vmem], ou...]
    all_to_all x1 -> x0, waiting for transfers between devices: 2.21 us -> none  [exchange(): lax.all_to_all(outgoing, ('cam', 'tile'), split_axis=0, concat_axis=0, ti...]
  transfers between devices with their start and end apart: 1 -> 0, of which waited for: 1 -> 0; matrix products, arithmetic and copies ran while one was open for 0% -> 0% of each run, Pallas kernels for 3% -> 0%
where the time goes in v2:
time: 142 us; the launch traced here: 141 us
  Pallas kernels  138 us (97%)
  local copies, waits for them, and re-layouts  2.25 us (2%)
    pallas_call x1, Pallas kernels, render(): pl.pallas_call(render_kernel, in_specs=[smem, smem, vmem, vmem, vmem], ou...  56.4 us
    pallas_call x1, Pallas kernels, collect(): pl.pallas_call(functools.partial(collect_kernel, *mesh_shape), in_specs=[...  27.1 us
    pallas_call x1, Pallas kernels, answer(): pl.pallas_call(functools.partial(answer_kernel, *mesh_shape), in_specs=[p...  23.1 us
    pallas_call x1, Pallas kernels, ask_and_project(): pl.pallas_call(functools.partial(ask_kernel, *mesh_shape), in_specs=[smem...  16.9 us
    pallas_call x1, Pallas kernels, apply_adam(): pl.pallas_call(adam_kernel, grid=(own_count // columns,), in_specs=[pl.Bl...  14.7 us

profile of v2, /device:TPU:1, one launch (start us, length us, event | category | flops | bytes accessed | tf_op | source)
XLA Modules:
  0.0 141.2 jit_solution(11200348930347084809)
XLA Ops:
  0.6 0.0 copy-start.1
  0.6 0.0 copy-start.2
  0.7 0.9 copy-done.2
  1.5 0.0 copy-start.4
  1.5 0.7 copy-done.4
  2.2 0.0 copy-start.5
  2.2 0.7 copy-done.5
  2.9 0.0 copy-start.3
  2.9 0.0 copy-start.6
  2.9 0.0 copy-start.7
  2.9 16.9 %ask_and_project.1 = (s32[128,1,128]{2,1,0:T(1,128)S(1)}, bf16[4,9,64,512]{3,2,1,0:T(8,128)(2,1)S(1)}, bf16[4,2,64,256]{3,2,1,0:T(8,128)(2,1)S(1)}) custom-call(f32[4,3]{1,0:T(4,128)S(1)} %copy-done.4, f32[4,3]{1,0:T(4,128)S(1)} %copy-done.5, s32[128,1,128]{2,1,0:T(1,128)S(1)} %bitcast.11, f32[59,16384]{1,0:T(8,128)} %params_ref.3), custom_call_target="tpu_custom_call" | custom-call | tf_op jit(solution)/shard_map/ask_and_project/pallas_call | solution.py:322
  19.8 0.0 copy-start
  19.8 23.1 %answer.1 = f32[128,16,128]{2,1,0:T(8,128)S(1)} custom-call(s32[128,1,128]{2,1,0:T(1,128)S(1)} %get-tuple-element.12.wanted_ref, bf16[4,9,64,512]{3,2,1,0:T(8,128)(2,1)S(1)} %get-tuple-element.13.table_ref, bf16[4,2,64,256]{3,2,1,0:T(8,128)(2,1)S(1)} %get-tuple-element.14.low_ref), custom_call_target="tpu_custom_call" | custom-call | tf_op jit(solution)/shard_map/answer/pallas_call | solution.py:408
  43.0 0.0 copy-done.1
  43.0 0.0 copy-done.3
  43.0 0.0 copy-done.6
  43.0 0.0 copy-done.7
  43.0 56.4 %render.1 = (f32[3,32,256]{2,1,0:T(8,128)}, f32[2048,128]{1,0:T(8,128)S(1)}) custom-call(s32[1,32]{1,0:T(1,128)S(1)} %copy-done.6, s32[1,32]{1,0:T(1,128)S(1)} %copy-done.7, f32[2048,128]{1,0:T(8,128)S(1)} %bitcast.8, s32[32,256]{1,0:T(8,128)S(1)} %bitcast.12, f32[3,32,256]{2,1,0:T(8,128)S(1)} %bitcast.10), custom_call_target="tpu_custom_call" | custom-call | tf_op jit(solution)/shard_map/render/pallas_call | solution.py:563
  99.4 27.1 %collect.1.pulls_ref = f32[10,128,128]{2,1,0:T(8,128)S(1)} custom-call(s32[128,1,128]{2,1,0:T(1,128)S(1)} %get-tuple-element.12.wanted_ref, f32[128,16,128]{2,1,0:T(8,128)S(1)} %bitcast.9), custom_call_target="tpu_custom_call" | custom-call | tf_op jit(solution)/shard_map/collect/pallas_call | solution.py:644
  126.5 0.0 copy-done
  126.5 14.7 %apply_adam.1 = (f32[59,16384]{1,0:T(8,128)}, f32[59,16384]{1,0:T(8,128)}, f32[59,16384]{1,0:T(8,128)}) custom-call(f32[4,3]{1,0:T(4,128)S(1)} %copy-done.4, f32[4,3]{1,0:T(4,128)S(1)} %copy-done.5, f32[10,128,128]{2,1,0:T(8,128)S(1)} %collect.1.pulls_ref, f32[59,16384]{1,0:T(8,128)S(1)} %copy-done, f32[59,16384]{1,0:T(8,128)} %one_ref.1, f32[59,16384]{1,0:T(8,128)} %two_ref.1), custom_call_target="tpu_custom_call" | custom-call | tf_op jit(solution)/shard_map/apply_adam/pallas_call | solution.py:714
Async XLA Ops:
  0.6 42.3 %copy-start.1 = (f32[3,1,32,256]{3,2,1,0:T(8,128)S(1)}, f32[3,1,32,256]{3,2,1,0:T(8,128)}, u32[]{:S(2)}) copy-start(f32[3,1,32,256]{3,2,1,0:T(8,128)} %param.19) | copy-start | bytes 294916
  0.6 0.9 copy-start.2
  1.5 0.7 copy-start.4
  2.2 0.7 copy-start.5
  2.9 40.1 %copy-start.3 = (s32[1,32,256]{2,1,0:T(8,128)S(1)}, s32[1,32,256]{2,1,0:T(8,128)}, u32[]{:S(2)}) copy-start(s32[1,32,256]{2,1,0:T(8,128)} %param.16) | copy-start | bytes 98308
  2.9 40.1 %copy-start.6 = (s32[1,32]{1,0:T(1,128)S(1)}, s32[1,32]{1,0:T(1,128)}, u32[]{:S(2)}) copy-start(s32[1,32]{1,0:T(1,128)} %counts_ref.1) | copy-start | bytes 388
  2.9 40.1 %copy-start.7 = (s32[1,32]{1,0:T(1,128)S(1)}, s32[1,32]{1,0:T(1,128)}, u32[]{:S(2)}) copy-start(s32[1,32]{1,0:T(1,128)} %ids_ref.1) | copy-start | bytes 388
  19.8 106.7 %copy-start = (f32[59,16384]{1,0:T(8,128)S(1)}, f32[59,16384]{1,0:T(8,128)}, u32[]{:S(2)}) copy-start(f32[59,16384]{1,0:T(8,128)} %params_ref.3) | copy-start | bytes 11599876

commit v3 on v2

--- a/solution.py
+++ b/solution.py
@@ -89,6 +89,8 @@
 WIDE = 256
 LANES = 128
 BIG = 3e38
+BY_LANES = (0, 1, 8)
+BY_MATRIX = (2, 3, 4, 5, 6, 7)
 DEAD = -1e4
 KEEP_MIN = 2.0**-24
 BF = jnp.bfloat16
@@ -204,26 +206,48 @@
     return pick, jnp.where(few == narrow, 1.0, 0.0)
 
 
-def pick_from(table, low_table, index):
+def matrix_pick(table, rows, index):
     pick, mask = one_hots(index)
-    spread = nn_dot(table, jnp.concatenate([pick, pick], axis=0))
-    extra = nn_dot(low_table, pick)
-    picked = []
-    for r in range(9):
-        part = spread[r * HALF : (r + 1) * HALF]
-        if r < 2:
-            part = part + extra[r * HALF : (r + 1) * HALF]
-        picked.append(jnp.sum(part * mask, axis=0, keepdims=True))
-    return picked
+    spread = nn_dot(table, pick)
+    low = rows * HALF
+    return [
+        jnp.sum(
+            (spread[r * HALF : (r + 1) * HALF] + spread[low + r * HALF : low + (r + 1) * HALF]) * mask,
+            axis=0,
+            keepdims=True,
+        )
+        for r in range(rows)
+    ]
+
+
+def lane_pick(loads, blocks, index):
+    lanes = jnp.broadcast_to(index & 127, (8, LANES))
+    level = index >> 10
+    spot = lax.broadcasted_iota(jnp.int32, (8, LANES), 0) == ((index >> 7) & 7)
+    bits = []
+    while 2 ** len(bits) < blocks:
+        bits.append(jnp.broadcast_to((level & 2 ** len(bits)) != 0, (8, LANES)))
+
+    def tree(load, first, depth):
+        if depth == 0:
+            return jnp.take_along_axis(load(first), lanes, axis=1, mode="promise_in_bounds")
+        half = 2 ** (depth - 1)
+        return jnp.where(
+            bits[depth - 1], tree(load, first + half, depth - 1), tree(load, first, depth - 1)
+        )
+
+    return [
+        jnp.sum(jnp.where(spot, tree(load, 0, len(bits)), 0.0), axis=0, keepdims=True) for load in loads
+    ]
 
 
 def put_into(rows, index):
     pick, mask = one_hots(index)
     mask = mask.astype(BF)
     parts = [two_parts(row) for row in rows]
-    high = jnp.concatenate([mask * part[0] for part in parts], axis=0)
-    low = jnp.concatenate([mask * part[1] for part in parts], axis=0)
-    return nt_dot(jnp.concatenate([high, low], axis=1), jnp.concatenate([pick, pick], axis=1))
+    placed = nt_dot(jnp.concatenate([mask * part[k] for k in range(2) for part in parts], axis=0), pick)
+    low = len(rows) * HALF
+    return placed[:low] + placed[low:]
 
 
 MESH = pl.DeviceIdType.MESH
@@ -244,7 +268,7 @@
         lax.fori_loop(1 if step == 0 else 0, tiles, tell, 0, unroll=4)
 
 
-def project_block(turn_ref, shift_ref, params_ref, table_ref, low_ref, half, step, columns):
+def project_block(turn_ref, shift_ref, params_ref, table_ref, exact_ref, half, step, columns):
     rows = columns // LANES
     start = pl.multiple_of(half * (HALF * LANES) + step * columns, columns)
     params = []
@@ -256,21 +280,21 @@
     opacity = jax.nn.sigmoid(params[10])
     at = half * LANES
     place = pl.ds(pl.multiple_of(step * rows, rows), rows)
+    far = pl.ds(pl.multiple_of(half * HALF + step * rows, rows), rows)
     for cam in range(4):
         matrix, eye = camera_of(turn_ref, shift_ref, cam, (rows, LANES))
         record = project(params, matrix, eye) + [opacity]
         for r, value in enumerate(record):
-            value = jnp.where(value == value, jnp.clip(value, -BIG, BIG), 0.0)
-            high, mid = two_parts(value)
-            table_ref[cam, r, place, at : at + LANES] = high
-            table_ref[cam, r, place, WIDE + at : WIDE + at + LANES] = mid
-            if r < 2:
-                low = (value - high.astype(F32)) - mid.astype(F32)
-                low_ref[cam, r, place, at : at + LANES] = low.astype(BF)
+            if r in BY_LANES:
+                exact_ref[cam, BY_LANES.index(r), far, :] = value
+            else:
+                value = jnp.where(value == value, jnp.clip(value, -BIG, BIG), 0.0)
+                for k, part in enumerate(two_parts(value)):
+                    table_ref[cam, k * len(BY_MATRIX) + BY_MATRIX.index(r), place, at : at + LANES] = part
 
 
 def ask_kernel(
-    cams, tiles, turn_ref, shift_ref, fetch_ref, params_ref, wanted_ref, table_ref, low_ref,
+    cams, tiles, turn_ref, shift_ref, fetch_ref, params_ref, wanted_ref, table_ref, exact_ref,
     held_ref, send_sem, recv_sem, own_sem, load_sem,
 ):
     columns = 2048
@@ -306,7 +330,7 @@
 
     def body(step, carry):
         for half in range(2):
-            project_block(turn_ref, shift_ref, held_ref, table_ref, low_ref, half, step, columns)
+            project_block(turn_ref, shift_ref, held_ref, table_ref, exact_ref, half, step, columns)
         return carry
 
     lax.fori_loop(0, steps, body, 0)
@@ -325,8 +349,8 @@
         out_specs=[vmem] * 3,
         out_shape=[
             jax.ShapeDtypeStruct(fetch.shape, jnp.int32),
-            jax.ShapeDtypeStruct((4, 9, HALF, 2 * WIDE), BF),
-            jax.ShapeDtypeStruct((4, 2, HALF, WIDE), BF),
+            jax.ShapeDtypeStruct((4, 2 * len(BY_MATRIX), HALF, WIDE), BF),
+            jax.ShapeDtypeStruct((4, len(BY_LANES), 2 * HALF, LANES), F32),
         ],
         scratch_shapes=[pltpu.VMEM(splat_params.shape, F32)] + [pltpu.SemaphoreType.DMA(())] * 4,
         compiler_params=pltpu.CompilerParams(
@@ -340,7 +364,7 @@
     return jnp.concatenate([ref[2 * chip], ref[2 * chip + 1]], axis=1)
 
 
-def answer_kernel(cams, tiles, wanted_ref, table_ref, low_ref, got_ref, held_ref, send_sem, recv_sem, own_sem):
+def answer_kernel(cams, tiles, wanted_ref, table_ref, exact_ref, got_ref, held_ref, send_sem, recv_sem, own_sem):
     chips = cams * tiles // 2
     per_cam = chips // cams
     others = 2 * chips - 1
@@ -351,14 +375,16 @@
     signal_all(barrier, cams, tiles)
 
     def fill(chip):
-        picked = pick_from(
-            table_ref[chip // per_cam].reshape(9 * HALF, 2 * WIDE),
-            low_ref[chip // per_cam].reshape(2 * HALF, WIDE),
-            pair_of(wanted_ref, chip),
+        cam = chip // per_cam
+        loads = [lambda v, r=r: exact_ref[cam, r, 8 * v : 8 * v + 8, :] for r in range(len(BY_LANES))]
+        count = len(BY_MATRIX)
+        middle = matrix_pick(
+            table_ref[cam].reshape(2 * count * HALF, WIDE), count, pair_of(wanted_ref, chip)
         )
-        block = jnp.concatenate(picked, axis=0)
-        held_ref[2 * chip, 0:9, :] = block[:, :LANES]
-        held_ref[2 * chip + 1, 0:9, :] = block[:, LANES:]
+        for k in range(2):
+            ends = lane_pick(loads, 2 * HALF // 8, wanted_ref[2 * chip + k])
+            rows = [part[:, k * LANES : (k + 1) * LANES] for part in middle]
+            held_ref[2 * chip + k, 0:9, :] = jnp.concatenate(ends[:2] + rows + ends[2:], axis=0)
 
     def send(other):
         pltpu.make_async_remote_copy(
@@ -402,7 +428,7 @@
     pltpu.make_async_copy(held_ref.at[many, 0:9], got_ref.at[many, 0:9], recv_sem).wait()
 
 
-def answer(mesh_shape, wanted, table, low):
+def answer(mesh_shape, wanted, table, exact):
     devices, _, capacity = wanted.shape
     shape = (devices, 16, capacity)
     return pl.pallas_call(
@@ -415,47 +441,44 @@
             vmem_limit_bytes=48 << 20, collective_id=1, has_side_effects=True
         ),
         name="answer",
-    )(wanted, table, low)
+    )(wanted, table, exact)
 
 
 def render_kernel(
     counts_ref, ids_ref, got_ref, lists_ref, goal_ref, image_ref, grads_ref,
-    table_ref, low_ref, before_ref, after_ref, total_ref,
+    table_ref, before_ref, after_ref, total_ref,
 ):
     tiles, entries = lists_ref.shape
     pixels = goal_ref.shape[2]
 
-    for h in range(2):
-        for r in range(9):
-            value = jnp.concatenate(
-                [got_ref[pl.ds((h * HALF + i) * 16 + r, 8, stride=16), :] for i in range(0, HALF, 8)], axis=0
-            )
-            high, mid = two_parts(value)
-            table_ref[r * HALF : (r + 1) * HALF, h * LANES : (h + 1) * LANES] = high
-            table_ref[r * HALF : (r + 1) * HALF, WIDE + h * LANES : WIDE + (h + 1) * LANES] = mid
-            if r < 2:
-                low = (value - high.astype(F32)) - mid.astype(F32)
-                low_ref[r * HALF : (r + 1) * HALF, h * LANES : (h + 1) * LANES] = low.astype(BF)
-    row = lax.broadcasted_iota(jnp.int32, (entries, entries), 0)
+    for r in range(9):
+        for i in range(0, 2 * HALF, 8):
+            table_ref[r * 2 * HALF + i : r * 2 * HALF + i + 8, :] = got_ref[pl.ds(i * 16 + r, 8, stride=16), :]
+    row = lax.broadcasted_iota(jnp.int32, (entries, entries), 0) & 127
     col = lax.broadcasted_iota(jnp.int32, (entries, entries), 1)
     before_ref[...] = jnp.where(row < col, 1.0, 0.0).astype(BF)
-    after_ref[...] = jnp.where(row > col, 1.0, 0.0).astype(BF)
+    after_ref[...] = jnp.where((row > col) | (col >= LANES), 1.0, 0.0).astype(BF)
     total_ref[...] = jnp.zeros_like(total_ref)
 
-    def tile_step(tile):
+    def opening(tile):
         index = lists_ref[pl.ds(tile, 1), :]
         live = lax.broadcasted_iota(jnp.int32, (1, entries), 1) < counts_ref[0, tile]
         number = ids_ref[0, tile]
         origin_x = ((number & 31) * TILE_PX + TILE_PX // 2).astype(F32)
         origin_y = ((number >> 5) * TILE_PX + TILE_PX // 2).astype(F32)
-        rec = pick_from(table_ref[...], low_ref[...], index)
+        loads = [
+            lambda v, r=r: table_ref[r * 2 * HALF + 8 * v : r * 2 * HALF + 8 * v + 8, :] for r in range(9)
+        ]
+        left = lane_pick(loads, 2 * HALF // 8, index[:, :LANES])
+        right = lane_pick(loads, 2 * HALF // 8, index[:, LANES:])
+        rec = [jnp.concatenate([left[r], right[r]], axis=1) for r in range(9)]
         rec_u = jnp.where(live, rec[0] - origin_x, 0.0)
         rec_v = jnp.where(live, rec[1] - origin_y, 0.0)
         con_a = jnp.where(live, rec[2], 0.0)
         con_b = jnp.where(live, rec[3], 0.0)
         con_c = jnp.where(live, rec[4], 0.0)
         log_o = jnp.where(live, jnp.maximum(jnp.log(rec[8]) * LOG2E, DEAD), DEAD)
-        colours = rec[5:8]
+        colours = [jnp.where(live, c, 0.0) for c in rec[5:8]]
 
         spot = lax.broadcasted_iota(jnp.int32, (TILE_PX, entries), 0).astype(F32) - 7.5
         off_x = spot - rec_u
@@ -468,10 +491,21 @@
         )
         alphas = jnp.exp2(power)
         log_keep = jnp.log(jnp.maximum(1.0 - alphas, KEEP_MIN))
-        log_high, log_low = two_parts(log_keep)
-        before = before_ref[...]
-        after = after_ref[...]
-        ahead = nn_dot(log_high, before) + nn_dot(log_low, before)
+        return index, rec_u, rec_v, con_a, con_b, con_c, colours, power, alphas, log_keep
+
+    def running(values, mask):
+        parts = [two_parts(value) for value in values]
+        sides = (slice(0, LANES), slice(LANES, 2 * LANES))
+        stacked = [
+            jnp.concatenate([part[0][:, side], part[1][:, side]], axis=1) for part in parts for side in sides
+        ]
+        sums = nn_dot(jnp.concatenate(stacked, axis=0), mask)
+        rows = values[0].shape[0]
+        return [
+            [sums[(2 * t + h) * rows : (2 * t + h + 1) * rows] for h in range(2)] for t in range(len(values))
+        ]
+
+    def painting(tile, colours, ahead, alphas):
         weights = jnp.exp(ahead) * alphas
         w_high, w_low = two_parts(weights)
 
@@ -501,8 +535,10 @@
             pull_one[c : c + 1] + (pull_one[3 + c : 4 + c] + pull_two[c : c + 1]) for c in range(3)
         ]
         share = weight_pull * weights
-        s_high, s_low = two_parts(share)
-        behind = nn_dot(s_high, after) + nn_dot(s_low, after)
+        return share, weights, col_grads
+
+    def closing(tile, index, rec_u, rec_v, con_a, con_b, con_c, power, log_keep, share, behind, col_grads):
+        spot = lax.broadcasted_iota(jnp.int32, (TILE_PX, entries), 0).astype(F32) - 7.5
         odds = jnp.exp2(power - log_keep * LOG2E)
         pull = share - odds * behind
 
@@ -543,11 +579,29 @@
         ]
         total_ref[...] += put_into(grads, index)
 
+    def tile_step(group):
+        opened = [opening(tile) for tile in group]
+        sums = running([o[9] for o in opened], before_ref[...])
+        aheads = [
+            jnp.concatenate([left[:, :LANES], right[:, :LANES] + left[:, LANES:]], axis=1)
+            for left, right in sums
+        ]
+        painted = [painting(t, o[6], a, o[8]) for t, o, a in zip(group, opened, aheads)]
+        sums = running([p[0] for p in painted], after_ref[...])
+        behinds = [
+            jnp.concatenate([left[:, :LANES] + right[:, LANES:], right[:, :LANES]], axis=1)
+            for left, right in sums
+        ]
+        for t, o, p, b in zip(group, opened, painted, behinds):
+            closing(t, *o[:6], o[7], o[9], p[0], b, p[2])
+
+    per_step = 4
+
     def body(step, carry):
-        tile_step(step)
+        tile_step([step * per_step + k for k in range(per_step)])
         return carry
 
-    lax.fori_loop(0, tiles, body, 0, unroll=2)
+    lax.fori_loop(0, tiles // per_step, body, 0)
     for h in range(2):
         for r in range(9):
             for i in range(0, HALF, 8):
@@ -569,8 +623,7 @@
             jax.ShapeDtypeStruct(got.shape, F32),
         ],
         scratch_shapes=[
-            pltpu.VMEM((9 * HALF, 2 * WIDE), BF),
-            pltpu.VMEM((2 * HALF, WIDE), BF),
+            pltpu.VMEM((18 * HALF, LANES), F32),
             pltpu.VMEM((entries, entries), BF),
             pltpu.VMEM((entries, entries), BF),
             pltpu.VMEM((9 * HALF, WIDE), F32),
@@ -743,10 +796,10 @@
 ):
     devices, capacity = fetch_table.shape[1:]
     mesh_shape = (lax.axis_size("cam"), lax.axis_size("tile"))
-    wanted, table, low = ask_and_project(
+    wanted, table, exact = ask_and_project(
         mesh_shape, fetch_table.reshape(devices, 1, capacity), splat_params, camera_turn, camera_shift
     )
-    arrived = answer(mesh_shape, wanted, table, low)
+    arrived = answer(mesh_shape, wanted, table, exact)
     rendered, slot_grads = render(
         tile_counts, tile_ids, arrived.reshape(devices * 16, capacity), tile_lists[0], target_image[:, 0]
     )

time: 142 us -> 119 us (0.84)
  Pallas kernels: 138 us -> 116 us
    pallas_call x1, Pallas kernels: 56.4 us -> 34.9 us  [render(): pl.pallas_call(render_kernel, in_specs=[smem, smem, vmem, vmem, vmem], ou...]
    pallas_call x1, Pallas kernels: 23.1 us -> 19.7 us  [answer(): pl.pallas_call(functools.partial(answer_kernel, *mesh_shape), in_specs=[p...]
    pallas_call x1, Pallas kernels: 27.1 us -> 29.8 us  [collect(): pl.pallas_call(functools.partial(collect_kernel, *mesh_shape), in_specs=[...]
where the time goes in v3:
time: 119 us
  Pallas kernels  116 us (97%)
  local copies, waits for them, and re-layouts  2.26 us (2%)
    pallas_call x1, Pallas kernels, render(): pl.pallas_call(render_kernel, in_specs=[smem, smem, vmem, vmem, vmem], ou...  34.9 us
    pallas_call x1, Pallas kernels, collect(): pl.pallas_call(functools.partial(collect_kernel, *mesh_shape), in_specs=[...  29.8 us
    pallas_call x1, Pallas kernels, answer(): pl.pallas_call(functools.partial(answer_kernel, *mesh_shape), in_specs=[p...  19.7 us
    pallas_call x1, Pallas kernels, ask_and_project(): pl.pallas_call(functools.partial(ask_kernel, *mesh_shape), in_specs=[smem...  16.8 us
    pallas_call x1, Pallas kernels, apply_adam(): pl.pallas_call(adam_kernel, grid=(own_count // columns,), in_specs=[pl.Bl...  14.7 us

profile of v3, /device:TPU:1, one launch (start us, length us, event | category | flops | bytes accessed | tf_op | source)
XLA Modules:
  0.0 118.9 jit_solution(13229945811698842353)
XLA Ops:
  0.6 0.0 copy-start.1
  0.6 0.0 copy-start.2
  0.7 0.9 copy-done.2
  1.5 0.0 copy-start.4
  1.5 0.7 copy-done.4
  2.2 0.0 copy-start.5
  2.2 0.7 copy-done.5
  2.9 0.0 copy-start.3
  2.9 0.0 copy-start.7
  2.9 0.0 copy-start.8
  2.9 16.8 %ask_and_project.1 = (s32[128,1,128]{2,1,0:T(1,128)S(1)}, bf16[4,12,64,256]{3,2,1,0:T(8,128)(2,1)S(1)}, f32[4,3,128,128]{3,2,1,0:T(8,128)S(1)}) custom-call(f32[4,3]{1,0:T(4,128)S(1)} %copy-done.4, f32[4,3]{1,0:T(4,128)S(1)} %copy-done.5, s32[128,1,128]{2,1,0:T(1,128)S(1)} %bitcast.11, f32[59,16384]{1,0:T(8,128)} %params_ref.3), custom_call_target="tpu_custom_call" | custom-call | tf_op jit(solution)/shard_map/ask_and_project/pallas_call | solution.py:346
  19.7 0.0 copy-start
  19.7 0.0 copy-start.6
  19.7 19.7 %answer.1 = f32[128,16,128]{2,1,0:T(8,128)S(1)} custom-call(s32[128,1,128]{2,1,0:T(1,128)S(1)} %get-tuple-element.12.wanted_ref, bf16[4,12,64,256]{3,2,1,0:T(8,128)(2,1)S(1)} %get-tuple-element.13.table_ref, f32[4,3,128,128]{3,2,1,0:T(8,128)S(1)} %get-tuple-element.14.exact_ref), custom_call_target="tpu_custom_call" | custom-call | tf_op jit(solution)/shard_map/answer/pallas_call | solution.py:434
  39.5 0.0 copy-done.1
  39.5 0.0 copy-done.3
  39.5 0.0 copy-done.7
  39.5 0.0 copy-done.8
  39.5 34.9 %render.1 = (f32[3,32,256]{2,1,0:T(8,128)}, f32[2048,128]{1,0:T(8,128)S(1)}) custom-call(s32[1,32]{1,0:T(1,128)S(1)} %copy-done.7, s32[1,32]{1,0:T(1,128)S(1)} %copy-done.8, f32[2048,128]{1,0:T(8,128)S(1)} %bitcast.8, s32[32,256]{1,0:T(8,128)S(1)} %bitcast.12, f32[3,32,256]{2,1,0:T(8,128)S(1)} %bitcast.10), custom_call_target="tpu_custom_call" | custom-call | tf_op jit(solution)/shard_map/render/pallas_call | solution.py:617
  74.4 29.8 %collect.1.pulls_ref = f32[10,128,128]{2,1,0:T(8,128)S(1)} custom-call(s32[128,1,128]{2,1,0:T(1,128)S(1)} %get-tuple-element.12.wanted_ref, f32[128,16,128]{2,1,0:T(8,128)S(1)} %bitcast.9), custom_call_target="tpu_custom_call" | custom-call | tf_op jit(solution)/shard_map/collect/pallas_call | solution.py:697
  104.2 0.0 copy-done
  104.2 0.0 copy-done.6
  104.2 14.7 %apply_adam.1 = (f32[59,16384]{1,0:T(8,128)}, f32[59,16384]{1,0:T(8,128)}, f32[59,16384]{1,0:T(8,128)}) custom-call(f32[4,3]{1,0:T(4,128)S(1)} %copy-done.4, f32[4,3]{1,0:T(4,128)S(1)} %copy-done.6, f32[10,128,128]{2,1,0:T(8,128)S(1)} %collect.1.pulls_ref, f32[59,16384]{1,0:T(8,128)S(1)} %copy-done, f32[59,16384]{1,0:T(8,128)} %one_ref.1, f32[59,16384]{1,0:T(8,128)} %two_ref.1), custom_call_target="tpu_custom_call" | custom-call | tf_op jit(solution)/shard_map/apply_adam/pallas_call | solution.py:767
Async XLA Ops:
  0.6 38.9 %copy-start.1 = (f32[3,1,32,256]{3,2,1,0:T(8,128)S(1)}, f32[3,1,32,256]{3,2,1,0:T(8,128)}, u32[]{:S(2)}) copy-start(f32[3,1,32,256]{3,2,1,0:T(8,128)} %param.19) | copy-start | bytes 294916
  0.6 0.9 copy-start.2
  1.5 0.7 copy-start.4
  2.2 0.7 copy-start.5
  2.9 36.6 %copy-start.3 = (s32[1,32,256]{2,1,0:T(8,128)S(1)}, s32[1,32,256]{2,1,0:T(8,128)}, u32[]{:S(2)}) copy-start(s32[1,32,256]{2,1,0:T(8,128)} %param.16) | copy-start | bytes 98308
  2.9 36.6 %copy-start.7 = (s32[1,32]{1,0:T(1,128)S(1)}, s32[1,32]{1,0:T(1,128)}, u32[]{:S(2)}) copy-start(s32[1,32]{1,0:T(1,128)} %counts_ref.1) | copy-start | bytes 388
  2.9 36.6 %copy-start.8 = (s32[1,32]{1,0:T(1,128)S(1)}, s32[1,32]{1,0:T(1,128)}, u32[]{:S(2)}) copy-start(s32[1,32]{1,0:T(1,128)} %ids_ref.1) | copy-start | bytes 388
  19.7 84.5 %copy-start = (f32[59,16384]{1,0:T(8,128)S(1)}, f32[59,16384]{1,0:T(8,128)}, u32[]{:S(2)}) copy-start(f32[59,16384]{1,0:T(8,128)} %params_ref.3) | copy-start | bytes 11599876
  19.7 84.5 %copy-start.6 = (f32[4,3]{1,0:T(4,128)S(1)}, f32[4,3]{1,0:T(4,128)}, u32[]{:S(2)}) copy-start(f32[4,3]{1,0:T(4,128)} %shift_ref.3) | copy-start | bytes 148

commit v4 on v3

--- a/solution.py
+++ b/solution.py
@@ -93,27 +93,62 @@
 BY_MATRIX = (2, 3, 4, 5, 6, 7)
 DEAD = -1e4
 KEEP_MIN = 2.0**-24
+EARLY_STEPS = 2
 BF = jnp.bfloat16
 F32 = jnp.float32
 
 
+@jax.custom_vjp
+def inverse(value):
+    return 1.0 / value
+
+
+def inverse_fwd(value):
+    result = 1.0 / value
+    return result, result
+
+
+def inverse_bwd(result, pull):
+    return (-pull * result * result,)
+
+
+inverse.defvjp(inverse_fwd, inverse_bwd)
+
+
+@jax.custom_vjp
+def inverse_root(value):
+    return 1.0 / jnp.sqrt(value)
+
+
+def inverse_root_fwd(value):
+    result = 1.0 / jnp.sqrt(value)
+    return result, result
+
+
+def inverse_root_bwd(result, pull):
+    return (-0.5 * pull * result * (result * result),)
+
+
+inverse_root.defvjp(inverse_root_fwd, inverse_root_bwd)
+
+
 def project(params, camera, eye_pos):
     scales = [jnp.exp(params[3 + i]) for i in range(3)]
-    norm_quat = jnp.sqrt(
+    inv_norm = inverse_root(
         params[6] * params[6]
         + params[7] * params[7]
         + params[8] * params[8]
         + params[9] * params[9]
     )
     rotation = quat_matrix(
-        params[6] / norm_quat, params[7] / norm_quat, params[8] / norm_quat, params[9] / norm_quat
+        params[6] * inv_norm, params[7] * inv_norm, params[8] * inv_norm, params[9] * inv_norm
     )
     relative = [params[i] - eye_pos[i] for i in range(3)]
     in_view = [
         camera[i][0] * relative[0] + camera[i][1] * relative[1] + camera[i][2] * relative[2]
         for i in range(3)
     ]
-    inv_depth = 1.0 / in_view[2]
+    inv_depth = inverse(in_view[2])
     screen_x = FOCAL * in_view[0] * inv_depth + CENTRE
     screen_y = FOCAL * in_view[1] * inv_depth + CENTRE
     axes_cam = [
@@ -135,8 +170,8 @@
     cov_xx = row_x[0] * row_x[0] + row_x[1] * row_x[1] + row_x[2] * row_x[2] + DILATION
     cov_xy = row_x[0] * row_y[0] + row_x[1] * row_y[1] + row_x[2] * row_y[2]
     cov_yy = row_y[0] * row_y[0] + row_y[1] * row_y[1] + row_y[2] * row_y[2] + DILATION
-    inv_det = 1.0 / (cov_xx * cov_yy - cov_xy * cov_xy)
-    inv_dist = 1.0 / jnp.sqrt(
+    inv_det = inverse(cov_xx * cov_yy - cov_xy * cov_xy)
+    inv_dist = inverse_root(
         relative[0] * relative[0] + relative[1] * relative[1] + relative[2] * relative[2]
     )
     basis = harmonics(relative[0] * inv_dist, relative[1] * inv_dist, relative[2] * inv_dist)
@@ -293,14 +328,10 @@
                     table_ref[cam, k * len(BY_MATRIX) + BY_MATRIX.index(r), place, at : at + LANES] = part
 
 
-def ask_kernel(
-    cams, tiles, turn_ref, shift_ref, fetch_ref, params_ref, wanted_ref, table_ref, exact_ref,
-    held_ref, send_sem, recv_sem, own_sem, load_sem,
-):
+def ask_phase(cams, tiles, turn_ref, shift_ref, fetch_ref, params_ref, wanted_ref, table_ref, exact_ref,
+              ready, send_sem, recv_sem, own_sem):
     columns = 2048
     steps = HALF * LANES // columns
-    load = pltpu.make_async_copy(params_ref, held_ref, load_sem)
-    load.start()
     barrier = pltpu.get_barrier_semaphore()
     signal_all(barrier, cams, tiles)
     own_cam = lax.axis_index("cam")
@@ -309,6 +340,16 @@
     others = cams * tiles - 1
     own = pltpu.make_async_copy(fetch_ref.at[me], wanted_ref.at[me], own_sem)
     own.start()
+    for copy in ready:
+        copy.wait()
+
+    def body(step, carry):
+        for half in range(2):
+            project_block(turn_ref, shift_ref, params_ref, table_ref, exact_ref, half, step, columns)
+        return carry
+
+    early = EARLY_STEPS
+    lax.fori_loop(0, early, body, 0)
     pl.semaphore_wait(barrier, others)
     for hop in range(cams):
         cam = lax.rem(own_cam + hop, cams)
@@ -326,53 +367,24 @@
             return carry
 
         lax.fori_loop(1 if hop == 0 else 0, tiles, ask, 0, unroll=4)
-    load.wait()
-
-    def body(step, carry):
-        for half in range(2):
-            project_block(turn_ref, shift_ref, held_ref, table_ref, exact_ref, half, step, columns)
-        return carry
-
-    lax.fori_loop(0, steps, body, 0)
+    lax.fori_loop(early, steps, body, 0)
     own.wait()
     many = pl.ds(0, others)
     pltpu.make_async_copy(fetch_ref.at[many], wanted_ref.at[many], send_sem).wait()
     pltpu.make_async_copy(fetch_ref.at[many], wanted_ref.at[many], recv_sem).wait()
 
 
-def ask_and_project(mesh_shape, fetch, splat_params, camera_turn, camera_shift):
-    vmem = pl.BlockSpec(memory_space=pltpu.VMEM)
-    smem = pl.BlockSpec(memory_space=pltpu.SMEM)
-    return pl.pallas_call(
-        functools.partial(ask_kernel, *mesh_shape),
-        in_specs=[smem, smem, vmem, pl.BlockSpec(memory_space=pl.ANY)],
-        out_specs=[vmem] * 3,
-        out_shape=[
-            jax.ShapeDtypeStruct(fetch.shape, jnp.int32),
-            jax.ShapeDtypeStruct((4, 2 * len(BY_MATRIX), HALF, WIDE), BF),
-            jax.ShapeDtypeStruct((4, len(BY_LANES), 2 * HALF, LANES), F32),
-        ],
-        scratch_shapes=[pltpu.VMEM(splat_params.shape, F32)] + [pltpu.SemaphoreType.DMA(())] * 4,
-        compiler_params=pltpu.CompilerParams(
-            vmem_limit_bytes=48 << 20, collective_id=0, has_side_effects=True
-        ),
-        name="ask_and_project",
-    )(camera_turn, camera_shift, fetch, splat_params)
-
-
 def pair_of(ref, chip):
     return jnp.concatenate([ref[2 * chip], ref[2 * chip + 1]], axis=1)
 
 
-def answer_kernel(cams, tiles, wanted_ref, table_ref, exact_ref, got_ref, held_ref, send_sem, recv_sem, own_sem):
+def answer_phase(cams, tiles, wanted_ref, table_ref, exact_ref, got_ref, held_ref, send_sem, recv_sem, own_sem):
     chips = cams * tiles // 2
     per_cam = chips // cams
     others = 2 * chips - 1
     me = lax.axis_index("cam") * tiles + lax.axis_index("tile")
     own_chip = me // 2
     twin = 2 * own_chip + (1 - lax.rem(me, 2))
-    barrier = pltpu.get_barrier_semaphore()
-    signal_all(barrier, cams, tiles)
 
     def fill(chip):
         cam = chip // per_cam
@@ -410,7 +422,6 @@
     fill_batch(0)
     own = pltpu.make_async_copy(held_ref.at[me, 0:9], got_ref.at[me, 0:9], own_sem)
     own.start()
-    pl.semaphore_wait(barrier, others)
     send(twin)
     for k in range(1, per_batch):
         send_chip(k)
@@ -428,23 +439,7 @@
     pltpu.make_async_copy(held_ref.at[many, 0:9], got_ref.at[many, 0:9], recv_sem).wait()
 
 
-def answer(mesh_shape, wanted, table, exact):
-    devices, _, capacity = wanted.shape
-    shape = (devices, 16, capacity)
-    return pl.pallas_call(
-        functools.partial(answer_kernel, *mesh_shape),
-        in_specs=[pl.BlockSpec(memory_space=pltpu.VMEM)] * 3,
-        out_specs=pl.BlockSpec(memory_space=pltpu.VMEM),
-        out_shape=jax.ShapeDtypeStruct(shape, F32),
-        scratch_shapes=[pltpu.VMEM(shape, F32)] + [pltpu.SemaphoreType.DMA(())] * 3,
-        compiler_params=pltpu.CompilerParams(
-            vmem_limit_bytes=48 << 20, collective_id=1, has_side_effects=True
-        ),
-        name="answer",
-    )(wanted, table, exact)
-
-
-def render_kernel(
+def render_phase(
     counts_ref, ids_ref, got_ref, lists_ref, goal_ref, image_ref, grads_ref,
     table_ref, before_ref, after_ref, total_ref,
 ):
@@ -453,7 +448,7 @@
 
     for r in range(9):
         for i in range(0, 2 * HALF, 8):
-            table_ref[r * 2 * HALF + i : r * 2 * HALF + i + 8, :] = got_ref[pl.ds(i * 16 + r, 8, stride=16), :]
+            table_ref[r * 2 * HALF + i : r * 2 * HALF + i + 8, :] = jnp.concatenate([got_ref[i + k, r : r + 1, :] for k in range(8)], axis=0)
     row = lax.broadcasted_iota(jnp.int32, (entries, entries), 0) & 127
     col = lax.broadcasted_iota(jnp.int32, (entries, entries), 1)
     before_ref[...] = jnp.where(row < col, 1.0, 0.0).astype(BF)
@@ -595,61 +590,43 @@
         for t, o, p, b in zip(group, opened, painted, behinds):
             closing(t, *o[:6], o[7], o[9], p[0], b, p[2])
 
-    per_step = 4
+    per_step = 16
 
     def body(step, carry):
         tile_step([step * per_step + k for k in range(per_step)])
         return carry
 
     lax.fori_loop(0, tiles // per_step, body, 0)
-    for h in range(2):
-        for r in range(9):
-            for i in range(0, HALF, 8):
-                grads_ref[pl.ds((h * HALF + i) * 16 + r, 8, stride=16), :] = total_ref[
-                    r * HALF + i : r * HALF + i + 8, h * LANES : (h + 1) * LANES
-                ]
-
-
-def render(counts, ids, got, lists, goal):
-    tiles, entries = lists.shape
-    vmem = pl.BlockSpec(memory_space=pltpu.VMEM)
-    smem = pl.BlockSpec(memory_space=pltpu.SMEM)
-    return pl.pallas_call(
-        render_kernel,
-        in_specs=[smem, smem, vmem, vmem, vmem],
-        out_specs=[vmem, vmem],
-        out_shape=[
-            jax.ShapeDtypeStruct(goal.shape, F32),
-            jax.ShapeDtypeStruct(got.shape, F32),
-        ],
-        scratch_shapes=[
-            pltpu.VMEM((18 * HALF, LANES), F32),
-            pltpu.VMEM((entries, entries), BF),
-            pltpu.VMEM((entries, entries), BF),
-            pltpu.VMEM((9 * HALF, WIDE), F32),
-        ],
-        compiler_params=pltpu.CompilerParams(vmem_limit_bytes=48 << 20),
-        name="render",
-    )(counts, ids, got, lists, goal)
-
-
-def collect_kernel(
-    cams, tiles, wanted_ref, away_ref, out_ref, back_ref, total_ref, send_sem, recv_sem
+    def lay(step, carry):
+        start = pl.multiple_of(8 * step, 8)
+        for h in range(2):
+            block = [
+                total_ref[pl.ds(pl.multiple_of(r * HALF + start, 8), 8), h * LANES : (h + 1) * LANES]
+                for r in range(9)
+            ]
+            for k in range(8):
+                grads_ref[h * HALF + start + k, 0:9, :] = jnp.concatenate(
+                    [part[k : k + 1] for part in block], axis=0
+                )
+        return carry
+
+    lax.fori_loop(0, HALF // 8, lay, 0)
+
+
+def collect_phase(
+    cams, tiles, wanted_ref, away_ref, out_ref, back_ref, total_ref, send_sem, recv_sem, own_sem
 ):
     chips = cams * tiles // 2
     per_cam = chips // cams
-    per_group = 4
+    per_group = 8
     groups = chips // per_group
+    ahead = 2
     others = 2 * chips - 1
     me = lax.axis_index("cam") * tiles + lax.axis_index("tile")
     own_chip = me // 2
     twin = 2 * own_chip + (1 - lax.rem(me, 2))
-    barrier = pltpu.get_barrier_semaphore()
-    signal_all(barrier, cams, tiles)
-    own = pltpu.make_async_copy(away_ref.at[me, 0:9], back_ref.at[me, 0:9], recv_sem.at[0])
+    own = pltpu.make_async_copy(away_ref.at[me, 0:9], back_ref.at[me, 0:9], own_sem)
     own.start()
-    total_ref[...] = jnp.zeros_like(total_ref)
-    pl.semaphore_wait(barrier, others)
 
     def send(other, group):
         pltpu.make_async_remote_copy(
@@ -661,28 +638,47 @@
             device_id_type=MESH,
         ).start()
 
+    def send_group(group, first):
+        for k in range(first, per_group):
+            chip = lax.rem(own_chip + group * per_group + k, chips)
+            send(2 * chip, group)
+            send(2 * chip + 1, group)
+
     send(twin, 0)
-
-    def give(step, carry):
-        chip = lax.rem(own_chip + step, chips)
-        send(2 * chip, step // per_group)
-        send(2 * chip + 1, step // per_group)
-        return carry
-
-    lax.fori_loop(1, chips, give, 0, unroll=3)
-
-    def take(group, carry):
-        block = pl.ds(0, 2 * per_group)
-        pltpu.make_async_copy(away_ref.at[block, 0:9], back_ref.at[block, 0:9], recv_sem.at[group]).wait()
+    send_group(0, 1)
+    for group in range(1, ahead):
+        send_group(group, 0)
+    total_ref[...] = jnp.zeros_like(total_ref)
+    own.wait()
+
+    def add_group(group):
         for k in range(per_group):
             chip = lax.rem(own_chip + chips - (group * per_group + k), chips)
             both = jnp.concatenate([back_ref[2 * chip, 0:9, :], back_ref[2 * chip + 1, 0:9, :]], axis=1)
             viewer = jnp.full((1, WIDE), chip // per_cam, jnp.int32).astype(F32)
             rows = [both[r : r + 1] for r in range(9)] + [viewer]
             total_ref[...] += put_into(rows, pair_of(wanted_ref, chip))
+
+    def arrive(group, count):
+        block = pl.ds(0, count)
+        pltpu.make_async_copy(away_ref.at[block, 0:9], back_ref.at[block, 0:9], recv_sem.at[group]).wait()
+
+    def take_and_send(group, carry):
+        send_group(group + ahead, 0)
+        arrive(group, 2 * per_group)
+        add_group(group)
         return carry
 
-    lax.fori_loop(0, groups, take, 0)
+    def take(group, carry):
+        arrive(group, 2 * per_group)
+        add_group(group)
+        return carry
+
+    arrive(0, 2 * per_group - 1)
+    send_group(ahead, 0)
+    add_group(0)
+    lax.fori_loop(1, groups - ahead, take_and_send, 0)
+    lax.fori_loop(groups - ahead, groups, take, 0)
     for r in range(10):
         for h in range(2):
             out_ref[r, h * HALF : (h + 1) * HALF, :] = total_ref[
@@ -692,24 +688,94 @@
     pltpu.make_async_copy(away_ref.at[many, 0:9], back_ref.at[many, 0:9], send_sem).wait()
 
 
-def collect(mesh_shape, wanted, away):
-    chips = mesh_shape[0] * mesh_shape[1] // 2
+def work_kernel(
+    cams, tiles, turn_hbm, shift_hbm, counts_hbm, ids_hbm, fetch_hbm, params_hbm, lists_hbm, goal_hbm,
+    image_ref, pulls_ref,
+    turn_ref, shift_ref, counts_ref, ids_ref, params_ref, lists_ref, goal_ref,
+    wanted_ref, table_ref, exact_ref, held_ref, got_ref, spread_ref, before_ref, after_ref, slots_ref,
+    away_ref, back_ref, total_ref, load_sems, send_sems, recv_sems, own_sems, group_sems,
+):
+    loads = [
+        pltpu.make_async_copy(source, target, load_sems.at[k])
+        for k, (source, target) in enumerate(
+            [
+                (params_hbm, params_ref),
+                (turn_hbm, turn_ref),
+                (shift_hbm, shift_ref),
+                (counts_hbm, counts_ref),
+                (ids_hbm, ids_ref),
+                (lists_hbm, lists_ref),
+                (goal_hbm, goal_ref),
+            ]
+        )
+    ]
+    for load in loads:
+        load.start()
+    ask_phase(
+        cams, tiles, turn_ref, shift_ref, fetch_hbm, params_ref, wanted_ref, table_ref, exact_ref,
+        loads[:3], send_sems.at[0], recv_sems.at[0], own_sems.at[0],
+    )
+    answer_phase(
+        cams, tiles, wanted_ref, table_ref, exact_ref, got_ref, held_ref,
+        send_sems.at[1], recv_sems.at[1], own_sems.at[1],
+    )
+    for load in loads[3:]:
+        load.wait()
+    render_phase(
+        counts_ref, ids_ref, got_ref, lists_ref, goal_ref, image_ref, away_ref,
+        spread_ref, before_ref, after_ref, slots_ref,
+    )
+    collect_phase(
+        cams, tiles, wanted_ref, away_ref, pulls_ref, back_ref, total_ref,
+        send_sems.at[2], group_sems, own_sems.at[2],
+    )
+
+
+def work(mesh_shape, turn, shift, counts, ids, fetch, params, lists, goal):
+    devices, _, capacity = fetch.shape
+    entries = lists.shape[1]
+    hbm = pl.BlockSpec(memory_space=pltpu.HBM)
+    vmem = pl.BlockSpec(memory_space=pltpu.VMEM)
+    blocks = pltpu.VMEM((devices, 16, capacity), F32)
     return pl.pallas_call(
-        functools.partial(collect_kernel, *mesh_shape),
-        in_specs=[pl.BlockSpec(memory_space=pltpu.VMEM)] * 2,
-        out_specs=pl.BlockSpec(memory_space=pltpu.VMEM),
-        out_shape=jax.ShapeDtypeStruct((10, 2 * HALF, LANES), F32),
+        functools.partial(work_kernel, *mesh_shape),
+        in_specs=[hbm] * 8,
+        out_specs=[vmem] * 2,
+        out_shape=[
+            jax.ShapeDtypeStruct(goal.shape, F32),
+            jax.ShapeDtypeStruct((10, 2 * HALF, LANES), F32),
+        ],
         scratch_shapes=[
-            pltpu.VMEM(away.shape, F32),
+            pltpu.SMEM(turn.shape, F32),
+            pltpu.SMEM(shift.shape, F32),
+            pltpu.SMEM(counts.shape, jnp.int32),
+            pltpu.SMEM(ids.shape, jnp.int32),
+            pltpu.VMEM(params.shape, F32),
+            pltpu.VMEM(lists.shape, jnp.int32),
+            pltpu.VMEM(goal.shape, F32),
+            pltpu.VMEM(fetch.shape, jnp.int32),
+            pltpu.VMEM((4, 2 * len(BY_MATRIX), HALF, WIDE), BF),
+            pltpu.VMEM((4, len(BY_LANES), 2 * HALF, LANES), F32),
+            blocks,
+            blocks,
+            pltpu.VMEM((18 * HALF, LANES), F32),
+            pltpu.VMEM((entries, entries), BF),
+            pltpu.VMEM((entries, entries), BF),
+            pltpu.VMEM((9 * HALF, WIDE), F32),
+            blocks,
+            blocks,
             pltpu.VMEM((10 * HALF, WIDE), F32),
-            pltpu.SemaphoreType.DMA(()),
-            pltpu.SemaphoreType.DMA((chips // 4,)),
+            pltpu.SemaphoreType.DMA((7,)),
+            pltpu.SemaphoreType.DMA((3,)),
+            pltpu.SemaphoreType.DMA((2,)),
+            pltpu.SemaphoreType.DMA((3,)),
+            pltpu.SemaphoreType.DMA((devices // 16,)),
         ],
         compiler_params=pltpu.CompilerParams(
-            vmem_limit_bytes=48 << 20, collective_id=2, has_side_effects=True
+            vmem_limit_bytes=52 << 20, collective_id=0, has_side_effects=True
         ),
-        name="collect",
-    )(wanted, away)
+        name="work",
+    )(*[pltpu.with_memory_space_constraint(x, pltpu.HBM) for x in (turn, shift, counts, ids, fetch, params, lists, goal)])
 
 
 def step_size(row):
@@ -726,18 +792,38 @@
     return 0.000125
 
 
-def adam_kernel(turn_ref, shift_ref, pulls_ref, params_ref, one_ref, two_ref, new_ref, new_one_ref, new_two_ref):
+def adam_kernel(
+    turn_hbm, shift_hbm, pulls_ref, painted_ref, params_ref, one_ref, two_ref,
+    new_ref, new_one_ref, new_two_ref, image_ref, turn_ref, shift_ref, view_ref, load_sems,
+):
     columns = params_ref.shape[1]
     total = params_ref.shape[0]
     rows = columns // LANES
+
+    @pl.when(pl.program_id(0) == 0)
+    def _():
+        loads = [
+            pltpu.make_async_copy(turn_hbm, turn_ref, load_sems.at[0]),
+            pltpu.make_async_copy(shift_hbm, shift_ref, load_sems.at[1]),
+        ]
+        for load in loads:
+            load.start()
+        image_ref[...] = painted_ref[...]
+        for load in loads:
+            load.wait()
+        for cam in range(4):
+            matrix, eye = camera_of(turn_ref, shift_ref, cam, (rows, LANES))
+            for k, value in enumerate(matrix[0] + matrix[1] + matrix[2] + eye):
+                view_ref[cam, k] = value
+
     params = dense_rows(params_ref, columns)
     viewer = pulls_ref[9]
-    matrix, eye = camera_of(turn_ref, shift_ref, 0, (rows, LANES))
+    view = [view_ref[0, k] for k in range(12)]
     for cam in range(1, 4):
         here = viewer > cam - 0.5
-        other, other_eye = camera_of(turn_ref, shift_ref, cam, (rows, LANES))
-        matrix = [[jnp.where(here, other[i][j], matrix[i][j]) for j in range(3)] for i in range(3)]
-        eye = [jnp.where(here, other_eye[i], eye[i]) for i in range(3)]
+        view = [jnp.where(here, view_ref[cam, k], view[k]) for k in range(12)]
+    matrix = [view[0:3], view[3:6], view[6:9]]
+    eye = view[9:12]
     _, pull_back = jax.vjp(lambda *values: project(values, matrix, eye), *params)
     grads = list(pull_back([pulls_ref[r] for r in range(8)]))
     grads[10] = pulls_ref[8] * jax.nn.sigmoid(-params[10])
@@ -755,31 +841,37 @@
                 rate = jnp.where(which >= k, sizes[k], rate)
         new_one_ref[at, :] = new_one
         new_two_ref[at, :] = new_two
-        new_ref[at, :] = params_ref[at, :] - rate * new_one / (
-            jnp.sqrt(new_two * (1.0 / BIAS_TWO)) + ADAM_EPS
-        )
-
-
-def apply_adam(pulls, params, one, two, camera_turn, camera_shift):
+        root = lax.rsqrt(new_two * (1.0 / BIAS_TWO))
+        new_ref[at, :] = params_ref[at, :] - (rate * new_one) * (root * (1.0 - ADAM_EPS * root))
+
+
+def apply_adam(pulls, painted, params, one, two, camera_turn, camera_shift):
     rows_in, own_count = params.shape
-    columns = 1024
+    columns = 4096
     block = pl.BlockSpec((rows_in, columns), lambda i: (0, i))
     return pl.pallas_call(
         adam_kernel,
         grid=(own_count // columns,),
         in_specs=[
-            pl.BlockSpec(memory_space=pltpu.SMEM),
-            pl.BlockSpec(memory_space=pltpu.SMEM),
+            pl.BlockSpec(memory_space=pltpu.HBM),
+            pl.BlockSpec(memory_space=pltpu.HBM),
             pl.BlockSpec((10, columns // LANES, LANES), lambda i: (0, i, 0)),
+            pl.BlockSpec(memory_space=pltpu.VMEM),
             block,
             block,
             block,
         ],
-        out_specs=[block] * 3,
-        out_shape=[jax.ShapeDtypeStruct(params.shape, F32)] * 3,
+        out_specs=[block] * 3 + [pl.BlockSpec(painted.shape, lambda i: (0, 0, 0))],
+        out_shape=[jax.ShapeDtypeStruct(params.shape, F32)] * 3 + [jax.ShapeDtypeStruct(painted.shape, F32)],
+        scratch_shapes=[
+            pltpu.SMEM(camera_turn.shape, F32),
+            pltpu.SMEM(camera_shift.shape, F32),
+            pltpu.VMEM((4, 12, columns // LANES, LANES), F32),
+            pltpu.SemaphoreType.DMA((2,)),
+        ],
         compiler_params=pltpu.CompilerParams(vmem_limit_bytes=48 << 20),
         name="apply_adam",
-    )(camera_turn, camera_shift, pulls, params, one, two)
+    )(camera_turn, camera_shift, pulls, painted, params, one, two)
 
 
 def shards(
@@ -796,16 +888,19 @@
 ):
     devices, capacity = fetch_table.shape[1:]
     mesh_shape = (lax.axis_size("cam"), lax.axis_size("tile"))
-    wanted, table, exact = ask_and_project(
-        mesh_shape, fetch_table.reshape(devices, 1, capacity), splat_params, camera_turn, camera_shift
+    painted, pulls = work(
+        mesh_shape,
+        camera_turn,
+        camera_shift,
+        tile_counts,
+        tile_ids,
+        fetch_table.reshape(devices, 1, capacity),
+        splat_params,
+        tile_lists[0],
+        target_image[:, 0],
     )
-    arrived = answer(mesh_shape, wanted, table, exact)
-    rendered, slot_grads = render(
-        tile_counts, tile_ids, arrived.reshape(devices * 16, capacity), tile_lists[0], target_image[:, 0]
-    )
-    pulls = collect(mesh_shape, wanted, slot_grads.reshape(devices, 16, capacity))
-    updated_params, updated_first, updated_second = apply_adam(
-        pulls, splat_params, first_moment, second_moment, camera_turn, camera_shift
+    updated_params, updated_first, updated_second, rendered = apply_adam(
+        pulls, painted, splat_params, first_moment, second_moment, camera_turn, camera_shift
     )
     return (updated_params, updated_first, updated_second, rendered[:, None])
 

time: 119 us -> 96.9 us (0.81)
  Pallas kernels: 116 us -> 95.9 us
  local copies, waits for them, and re-layouts: 2.26 us -> 0.01 us
    pallas_call x4 -> x1, Pallas kernels: 101 us -> 85.2 us  [work(): pl.pallas_call(functools.partial(work_kernel, *mesh_shape), in_specs=[hbm...]
    pallas_call x1, Pallas kernels: 14.7 us -> 10.6 us  [apply_adam(): pl.pallas_call(adam_kernel, grid=(own_count // columns,), in_specs=[pl.Bl...]
    unnamed x18 -> x6, local copies, waits for them, and re-layouts: 2.26 us -> 0.01 us
where the time goes in v4:
time: 96.9 us; the launch traced here: 96.7 us
  Pallas kernels  95.9 us (99%)
    pallas_call x1, Pallas kernels, work(): pl.pallas_call(functools.partial(work_kernel, *mesh_shape), in_specs=[hbm...  85.2 us
    pallas_call x1, Pallas kernels, apply_adam(): pl.pallas_call(adam_kernel, grid=(own_count // columns,), in_specs=[pl.Bl...  10.6 us

profile of v4, /device:TPU:1, one launch (start us, length us, event | category | flops | bytes accessed | tf_op | source)
XLA Modules:
  0.0 96.7 jit_solution(17708535349780990374)
XLA Ops:
  0.6 0.0 copy-start.2
  0.6 0.0 copy-start.1
  0.7 0.0 copy-start
  0.7 85.2 %work.1 = (f32[3,32,256]{2,1,0:T(8,128)S(1)}, f32[10,128,128]{2,1,0:T(8,128)S(1)}) custom-call(f32[4,3]{1,0:T(4,128)} %turn_hbm.3, f32[4,3]{1,0:T(4,128)} %shift_hbm.3, s32[1,32]{1,0:T(1,128)} %counts_hbm.1, s32[1,32]{1,0:T(1,128)} %ids_hbm.1, s32[128,1,128]{2,1,0:T(1,128)} %bitcast.7, f32[59,16384]{1,0:T(8,128)} %params_ref.1, s32[32,256]{1,0:T(8,128)} %bitcast.8, ...), custom_call_target="tpu_custom_call" | custom-call | tf_op jit(solution)/shard_map/work/pallas_call | solution.py:740
  85.9 0.0 copy-done.2
  85.9 0.0 copy-done.1
  85.9 0.0 copy-done
  85.9 10.6 %apply_adam.1 = (f32[59,16384]{1,0:T(8,128)}, f32[59,16384]{1,0:T(8,128)}, f32[59,16384]{1,0:T(8,128)}, f32[3,32,256]{2,1,0:T(8,128)}) custom-call(f32[4,3]{1,0:T(4,128)S(1)} %copy-done.1, f32[4,3]{1,0:T(4,128)S(1)} %copy-done.2, f32[10,128,128]{2,1,0:T(8,128)S(1)} %get-tuple-element.10.pulls_ref, f32[3,32,256]{2,1,0:T(8,128)S(1)} %get-tuple-element.11.painted_ref, ...), custom_call_target="tpu_custom_call" | custom-call | tf_op jit(solution)/shard_map/apply_adam/pallas_call | solution.py:852
Async XLA Ops:
  0.6 85.2 %copy-start.2 = (f32[4,3]{1,0:T(4,128)S(1)}, f32[4,3]{1,0:T(4,128)}, u32[]{:S(2)}) copy-start(f32[4,3]{1,0:T(4,128)} %shift_hbm.3) | copy-start | bytes 148
  0.6 85.2 %copy-start.1 = (f32[4,3]{1,0:T(4,128)S(1)}, f32[4,3]{1,0:T(4,128)}, u32[]{:S(2)}) copy-start(f32[4,3]{1,0:T(4,128)} %turn_hbm.3) | copy-start | bytes 148
  0.7 85.2 %copy-start = (f32[59,16384]{1,0:T(8,128)S(1)}, f32[59,16384]{1,0:T(8,128)}, u32[]{:S(2)}) copy-start(f32[59,16384]{1,0:T(8,128)} %params_ref.1) | copy-start | bytes 11599876

commit v5 on v4

--- a/solution.py
+++ b/solution.py
@@ -408,7 +408,7 @@
             device_id_type=MESH,
         ).start()
 
-    per_batch = 4
+    per_batch = 8
 
     def fill_batch(batch):
         for k in range(per_batch):

time: 96.9 us -> 96.6 us (level)
  no operation moved by 1% of the time
where the time goes in v5:
time: 96.6 us; the launch traced here: 96.5 us
  Pallas kernels  95.6 us (99%)
    pallas_call x1, Pallas kernels, work(): pl.pallas_call(functools.partial(work_kernel, *mesh_shape), in_specs=[hbm...  84.9 us
    pallas_call x1, Pallas kernels, apply_adam(): pl.pallas_call(adam_kernel, grid=(own_count // columns,), in_specs=[pl.Bl...  10.6 us

profile of v5, /device:TPU:1, one launch (start us, length us, event | category | flops | bytes accessed | tf_op | source)
XLA Modules:
  0.0 96.5 jit_solution(1790200656786710598)
XLA Ops:
  0.6 0.0 copy-start.2
  0.6 0.0 copy-start.1
  0.7 0.0 copy-start
  0.7 84.9 %work.1 = (f32[3,32,256]{2,1,0:T(8,128)S(1)}, f32[10,128,128]{2,1,0:T(8,128)S(1)}) custom-call(f32[4,3]{1,0:T(4,128)} %turn_hbm.3, f32[4,3]{1,0:T(4,128)} %shift_hbm.3, s32[1,32]{1,0:T(1,128)} %counts_hbm.1, s32[1,32]{1,0:T(1,128)} %ids_hbm.1, s32[128,1,128]{2,1,0:T(1,128)} %bitcast.7, f32[59,16384]{1,0:T(8,128)} %params_ref.1, s32[32,256]{1,0:T(8,128)} %bitcast.8, ...), custom_call_target="tpu_custom_call" | custom-call | tf_op jit(solution)/shard_map/work/pallas_call | solution.py:740
  85.6 0.0 copy-done.2
  85.6 0.0 copy-done.1
  85.6 0.0 copy-done
  85.6 10.6 %apply_adam.1 = (f32[59,16384]{1,0:T(8,128)}, f32[59,16384]{1,0:T(8,128)}, f32[59,16384]{1,0:T(8,128)}, f32[3,32,256]{2,1,0:T(8,128)}) custom-call(f32[4,3]{1,0:T(4,128)S(1)} %copy-done.1, f32[4,3]{1,0:T(4,128)S(1)} %copy-done.2, f32[10,128,128]{2,1,0:T(8,128)S(1)} %get-tuple-element.10.pulls_ref, f32[3,32,256]{2,1,0:T(8,128)S(1)} %get-tuple-element.11.painted_ref, ...), custom_call_target="tpu_custom_call" | custom-call | tf_op jit(solution)/shard_map/apply_adam/pallas_call | solution.py:852
Async XLA Ops:
  0.6 85.0 %copy-start.2 = (f32[4,3]{1,0:T(4,128)S(1)}, f32[4,3]{1,0:T(4,128)}, u32[]{:S(2)}) copy-start(f32[4,3]{1,0:T(4,128)} %shift_hbm.3) | copy-start | bytes 148
  0.6 85.0 %copy-start.1 = (f32[4,3]{1,0:T(4,128)S(1)}, f32[4,3]{1,0:T(4,128)}, u32[]{:S(2)}) copy-start(f32[4,3]{1,0:T(4,128)} %turn_hbm.3) | copy-start | bytes 148
  0.7 85.0 %copy-start = (f32[59,16384]{1,0:T(8,128)S(1)}, f32[59,16384]{1,0:T(8,128)}, u32[]{:S(2)}) copy-start(f32[59,16384]{1,0:T(8,128)} %params_ref.1) | copy-start | bytes 11599876
